TPU v7x, 32 devices: a whole 2x2x4 slice. The times are simulated.
32 devices in a mesh: groups: 1, ctx: 16 (over z, y, core), pipe: 2 (over x), dp: 1.
Axes of the slice: x: 2, y: 2, z: 4, core: 2. Of those that a mesh axis runs over, the one named last changes fastest.
Arguments:
- rows_in: bfloat16 [2, 1, 4096, 1024], P(('groups', 'pipe'), 'dp', 'ctx'), may hold values from -6 to 6
- queries: bfloat16 [2, 1, 4096, 1024], P(('groups', 'pipe'), 'dp', 'ctx'), may hold values from -6 to 6
- keys: bfloat16 [2, 1, 4096, 1024], P(('groups', 'pipe'), 'dp', 'ctx'), may hold values from -12 to 12
- strengths: float32 [2, 1, 8, 4096], P(('groups', 'pipe'), 'dp', None, 'ctx'), may hold values from 0.05 to 0.5
- gates: float32 [2, 1, 8, 4096], P(('groups', 'pipe'), 'dp', None, 'ctx'), may hold values from 0.45 to 1
- doc_ids: int32 [2, 1, 4096], P(('groups', 'pipe'), 'dp', 'ctx'), may hold values from 0 to 7, never falling along the last dimension, each value on 1 to 1024 neighbouring positions
- positives: int32 [2, 1, 8], P(('groups', 'pipe'), 'dp'), may hold values from 0 to 7, as said below
- norm_gain: float32 [2, 128], P('pipe'), may hold values from 0.5 to 1.5
Outputs:
- rows_next: bfloat16 [2, 1, 4096, 1024], P(('groups', 'pipe'), 'dp', 'ctx')
- doc_loss: float32 [2, 1, 8], P(('groups', 'pipe'), 'dp')
Inputs may be any that keep to these rules, and one draw needn't show every extreme that they name: `positives`: never the document's own index dp * 8 + its document number.
All inputs are finite; a program needn't handle non-finite values.
Results may differ from a plain program's by a relative error of at most 0.008.
Values may be sent and summed in bfloat16 or wider, within the bound.
No kernel may reach another device: no remote copies, remote signals or barrier semaphores. Data moves between devices by JAX's collectives and lax.ppermute only.
A program may use at most 128 MiB of HBM per device.

v0:
```python
import jax
import jax.numpy as jnp
from jax import lax
from jax.sharding import PartitionSpec as P


def from_behind(block, axis, distance):
    devices = range(lax.axis_size(axis))
    route = [(i - distance, i) for i in devices if i - distance in devices]
    return lax.ppermute(block, axis, route)


def entering(array, axis, combine, identity):
    size, place = (lax.axis_size(axis), lax.axis_index(axis))
    everything = jax.tree.map(
        lambda part, kind: lax.all_gather(part.astype(kind), axis),
        array,
        (jnp.bfloat16, jnp.bfloat16),
    )
    start = jax.tree.map(
        lambda part, zero: jnp.broadcast_to(jnp.asarray(zero, part.dtype), part.shape),
        array,
        identity,
    )

    def step(k, before):
        reached = k < place
        new = combine(
            before, jax.tree.map(lambda part, own: part[k].astype(own.dtype), everything, array)
        )
        return jax.tree.map(lambda a, b: jnp.where(reached, a, b), new, before)

    return lax.fori_loop(0, size, step, start)


def shifted(array, axis, by):
    size = lax.axis_size(axis)
    return lax.ppermute(array, axis, [(i, (i + by) % size) for i in range(size)])


def unit_rows(x):
    return x * lax.rsqrt(jnp.sum(x * x, axis=-1, keepdims=True) + 1e-06)


def on_device(rows_in, queries, keys, strengths, gates, doc_ids, positives, norm_gain):
    hi = lax.Precision.HIGHEST
    length = rows_in.shape[2]
    heads = strengths.shape[2]
    width = rows_in.shape[3] // heads
    ndoc = positives.shape[2]
    values = rows_in[0, 0].astype(jnp.float32).reshape(length, heads, width).transpose(1, 0, 2)
    qn = unit_rows(
        queries[0, 0].astype(jnp.float32).reshape(length, heads, width).transpose(1, 0, 2)
    )
    kn = unit_rows(keys[0, 0].astype(jnp.float32).reshape(length, heads, width).transpose(1, 0, 2))
    beta = strengths[0, 0]
    ids = doc_ids[0, 0]
    before = from_behind(ids[-1:], "ctx", 1)
    prior = jnp.concatenate([before, ids[:-1]])
    reset = (ids != prior).astype(jnp.int32)
    run = jnp.cumsum(reset)
    logsum = jnp.cumsum(jnp.log(gates[0, 0]), axis=1)
    rows_idx = jnp.arange(length)[:, None]
    cols_idx = jnp.arange(length)[None, :]
    same = (run[:, None] == run[None, :]) & (rows_idx >= cols_idx)
    expo = jnp.where(same[None], logsum[:, :, None] - logsum[:, None, :], -jnp.inf)
    decay = jnp.exp(expo)
    lead = jnp.exp(logsum) * (run == 0).astype(jnp.float32)[None, :]
    tail = decay[:, length - 1, :]
    lead_end = lead[:, length - 1]
    inner = jnp.einsum("hti,hsi->hts", kn, kn, precision=hi)
    lower = jnp.where((rows_idx > cols_idx)[None], beta[:, :, None] * decay * inner, 0.0)
    eye_long = jnp.eye(length, dtype=jnp.float32)
    system = lower + eye_long[None]
    rhs = jnp.concatenate([beta[..., None] * values, (beta * lead)[..., None] * kn], axis=2)
    solved = jax.scipy.linalg.solve_triangular(system, rhs, lower=True, unit_diagonal=True)
    wv = solved[:, :, :width]
    yy = solved[:, :, width:]
    kd = kn * tail[..., None]
    eye_small = jnp.eye(width, dtype=jnp.float32)
    pmat = lead_end[:, None, None] * eye_small[None] - jnp.einsum(
        "hti,htj->hij", kd, yy, precision=hi
    )
    umat = jnp.einsum("hti,htj->hij", kd, wv, precision=hi)

    def combine(earlier, later):
        first = jnp.einsum("hij,hjk->hik", later[0], earlier[0], precision=hi)
        second = jnp.einsum("hij,hjk->hik", later[0], earlier[1], precision=hi) + later[1]
        return (first, second)

    identity = (jnp.broadcast_to(eye_small, pmat.shape), jnp.zeros_like(umat))
    prefix = entering((pmat, umat), "ctx", combine, identity)
    state_in = prefix[1]
    writes = wv - jnp.einsum("hti,hij->htj", yy, state_in, precision=hi)
    attend = decay * jnp.einsum("hti,hsi->hts", qn, kn, precision=hi)
    outs = lead[..., None] * jnp.einsum("hti,hij->htj", qn, state_in, precision=hi)
    outs = outs + jnp.einsum("hts,hsj->htj", attend, writes, precision=hi)
    scale = lax.rsqrt(jnp.mean(outs * outs, axis=-1, keepdims=True) + 1e-06)
    normed = outs * scale * norm_gain[0][None, None, :]
    rows_out = (
        (values + normed).transpose(1, 0, 2).reshape(length, heads * width).astype(jnp.bfloat16)
    )
    passed = shifted(rows_out, "pipe", 1)
    onehot = (jnp.arange(ndoc, dtype=jnp.int32)[:, None] == ids[None, :]).astype(jnp.bfloat16)
    pooled = jnp.dot(onehot, rows_out, preferred_element_type=jnp.float32)
    replica = lax.axis_index("dp")
    replicas = lax.axis_size("dp")
    summed = lax.psum(pooled.astype(jnp.bfloat16), "ctx").astype(jnp.float32)
    mine = unit_rows(summed)
    cands = lax.all_gather(mine.astype(jnp.bfloat16), "dp", axis=0, tiled=True).astype(mine.dtype)
    scores = jnp.dot(mine, cands.T, precision=hi, preferred_element_type=jnp.float32) / 0.05
    cidx = jnp.arange(replicas * ndoc, dtype=jnp.int32)
    own = replica * ndoc + jnp.arange(ndoc, dtype=jnp.int32)
    total = jnp.sum(jnp.where(cidx[None, :] != own[:, None], jnp.exp(scores), 0.0), axis=-1)
    picked = jnp.sum(jnp.where(cidx[None, :] == positives[0, 0][:, None], scores, 0.0), axis=-1)
    doc_loss = (jnp.log(total) - picked).reshape(1, 1, ndoc)
    return (passed.reshape(1, 1, length, heads * width), doc_loss)


def solution(mesh):
    in_specs = (
        P(("groups", "pipe"), "dp", "ctx", None),
        P(("groups", "pipe"), "dp", "ctx", None),
        P(("groups", "pipe"), "dp", "ctx", None),
        P(("groups", "pipe"), "dp", None, "ctx"),
        P(("groups", "pipe"), "dp", None, "ctx"),
        P(("groups", "pipe"), "dp", "ctx"),
        P(("groups", "pipe"), "dp", None),
        P("pipe", None),
    )
    out_specs = (P(("groups", "pipe"), "dp", "ctx", None), P(("groups", "pipe"), "dp", None))
    return jax.shard_map(
        on_device, mesh=mesh, in_specs=in_specs, out_specs=out_specs, check_vma=False
    )
```

profile of v0, /device:TPU:0, one launch (start us, length us, event | category | flops | bytes accessed | tf_op | source)
XLA Modules:
  0.0 435.6 jit_solution(13908347986221242588)
XLA Ops:
  7.2 1.3 slice.54
  8.5 2.9 collective-permute-start
  11.5 1.2 copy.35
  15.1 1.2 copy.38
  16.3 1.6 bitcast_multiply_fusion.1
  19.5 1.7 select_exponential_fusion
  21.2 4.0 select_add_fusion
  25.2 8.1 %while.15 = (s32[]{:T(128)}, f32[8,256,256]{2,1,0:T(8,128)}, s32[2,2]{1,0:T(2,128)S(1)}, f32[2,8,128,128]{3,2,0,1:T(8,128)}, s32[]{:T(128)}) while((s32[]{:T(128)}, f32[8,256,256]{2,1,0:T(8,128)}, s32[2,2]{1,0:T(2,128)S(1)}, f32[2,8,128,128]{3,2,0,1:T(8,128)}, s32[]{:T(128)}) %tuple.60), condition=%wide.while_cond, body=%wide.while_body.sunk | while | flops 2 | bytes 1050209 | solution.py:76
  25.8 3.6 bitcast_dynamic-update-slice_fusion.2
  30.0 3.4 bitcast_dynamic-update-slice_fusion.2
  33.4 158.6 %custom-call.4 = f32[8,2,128,128]{2,3,1,0:T(8,128)} custom-call(f32[8,2,128,128]{3,2,1,0:T(8,128)} %bitcast.135), custom_call_target="InvertDiagBlocksLowerTriangular" | custom-call | tf_op jit(solution)/shard_map/jit(_solve_triangular)/vmap()/triangular_solve | solution.py:76
  194.3 2.1 convolution_subtract_fusion.1
  198.3 3.4 convolution_convert_fusion
  202.1 3.4 fusion.10
  205.5 1.1 convert_bitcast_fusion
  207.8 3.3 fusion.25
  211.2 43.2 %all-gather.7.cloned.1.call-done = bf16[128,128,128]{2,1,0:T(8,128)(2,1)} async-done(((bf16[8,128,128]{2,1,0:T(8,128)(2,1)}), bf16[128,128,128]{2,1,0:T(8,128)(2,1)}) %all-gather.7.cloned.1.call-update) | async-done | bytes 4194320 | tf_op jit(solution)/shard_map/all_gather | solution.py:16
  254.4 51.2 %all-gather.5.cloned.1.call-done = bf16[128,128,128]{2,1,0:T(8,128)(2,1)} async-done(((bf16[8,128,128]{2,1,0:T(8,128)(2,1)}), bf16[128,128,128]{2,1,0:T(8,128)(2,1)}) %all-gather.5.cloned.1.call-update) | async-done | bytes 4194320 | tf_op jit(solution)/shard_map/all_gather | solution.py:16
  305.6 53.4 %while.16 = (s32[]{:T(128)}, f32[8,128,128]{2,1,0:T(8,128)}, s32[]{:T(128)}, bf16[16,8,128,128]{3,2,1,0:T(8,128)(2,1)}, bf16[16,8,128,128]{3,2,1,0:T(8,128)(2,1)}, /*index=5*/s32[]{:T(128)}, s32[]{:T(128)}) while((s32[]{:T(128)}, f32[8,128,128]{2,1,0:T(8,128)}, s32[]{:T(128)}, bf16[16,8,128,128]{3,2,1,0:T(8,128)(2,1)}, ...), condition=%wide.region_7.8_spmd.clone, body=%wide.region_6.7_spmd.clone.sunk | while | flops 201981952 | bytes 3148383 | solution.py:33
  305.6 1.0 copy.89
  306.7 2.3 fusion.72
  309.0 1.0 copy.89
  310.0 2.3 fusion.72
  312.3 1.0 copy.89
  313.3 2.3 fusion.72
  315.6 1.0 copy.89
  316.7 2.3 fusion.72
  319.0 1.0 copy.89
  320.0 2.3 fusion.72
  322.3 1.0 copy.89
  323.4 2.3 fusion.72
  325.6 1.0 copy.89
  326.7 2.3 fusion.72
  329.0 1.0 copy.89
  330.0 2.3 fusion.72
  333.4 2.3 fusion.72
  336.7 2.3 fusion.72
  340.0 2.3 fusion.72
  343.4 2.3 fusion.72
  346.7 2.3 fusion.72
  350.0 2.3 fusion.72
  353.4 2.3 fusion.72
  356.7 2.3 fusion.72
  359.0 2.2 convolution_subtract_fusion
  361.3 1.5 fusion.26
  362.9 2.8 multiply_reduce_fusion
  366.2 1.5 collective-permute-start.1
  367.9 58.9 %psum.7 = bf16[8,1024]{1,0:T(8,128)(2,1)S(1)} all-reduce(bf16[8,1024]{1,0:T(8,128)(2,1)S(1)} %convolution_convert_fusion.1), channel_id=1, replica_groups=mesh['groups'=1,'ctx'=16,'pipe'=2,'dp'=1] {'ctx'}, use_global_device_ids=true, to_apply=%region_9.10 | all-reduce | flops 8192 | bytes 32768 | tf_op jit(solution)/shard_map/psum | solution.py:108
  (89 shorter events, 21.9 us)
Async XLA Ops:
  7.2 6.2 %copy-start.12 = (f32[1,1,8,256]{3,2,1,0:T(8,128)S(1)}, f32[1,1,8,256]{3,2,1,0:T(8,128)}, u32[]{:S(2)}) copy-start(f32[1,1,8,256]{3,2,1,0:T(8,128)} %param.14) | copy-start | bytes 24580
  7.2 7.7 %copy-start.7 = (bf16[1,1,256,1024]{3,2,1,0:T(8,128)(2,1)S(1)}, bf16[1,1,256,1024]{3,2,1,0:T(8,128)(2,1)}, u32[]{:S(2)}) copy-start(bf16[1,1,256,1024]{3,2,1,0:T(8,128)(2,1)} %param.10) | copy-start | bytes 1572868
  7.2 247.2 %all-gather.7.cloned.1.call-start = ((), (), s32[]{:S(2)}) async-start(), calls=%async_computation.1 | async-start | bytes 4456448 | tf_op jit(solution)/shard_map/all_gather | solution.py:16
  8.5 9.4 %collective-permute-start = (s32[1]{0:T(128)}, s32[1]{0:T(128)}, u32[]{:S(2)}, u32[]{:S(2)}) collective-permute-start(s32[1]{0:T(128)} %bitcast.4), channel_id=1, source_target_pairs={{0,2},{2,4},{4,6},{6,8},{8,10},{10,12},{12,14},{14,16},{16,18},{18... | collective-permute-start | bytes 20 | tf_op jit(solution)/shard_map/ppermute | solution.py:10
  13.0 3.3 copy-start.10
  15.1 6.1 %copy-start.4 = (bf16[1,1,256,1024]{2,3,1,0:T(8,128)(2,1)}, bf16[1,1,256,1024]{2,3,1,0:T(8,128)(2,1)S(1)}, u32[]{:S(2)}) copy-start(bf16[1,1,256,1024]{2,3,1,0:T(8,128)(2,1)S(1)} %copy.33) | copy-start | bytes 1572868
  15.1 2.8 copy-start.11
  16.3 4.9 %copy-start.8 = (pred[256,256]{1,0:T(8,128)(4,1)S(1)}, pred[256,256]{1,0:T(8,128)(4,1)}, u32[]{:S(2)}) copy-start(pred[256,256]{1,0:T(8,128)(4,1)} %get-tuple-element.157) | copy-start | bytes 196612
  16.3 4.9 %copy-start.9 = (pred[256,256]{1,0:T(8,128)(4,1)S(1)}, pred[256,256]{1,0:T(8,128)(4,1)}, u32[]{:S(2)}) copy-start(pred[256,256]{1,0:T(8,128)(4,1)} %get-tuple-element.158) | copy-start | bytes 196612
  192.0 1.2 copy-start.6
  201.7 104.0 %all-gather.5.cloned.1.call-start = ((), (), s32[]{:S(2)}) async-start(), calls=%async_computation | async-start | bytes 4456448 | tf_op jit(solution)/shard_map/all_gather | solution.py:16
  206.9 1.0 copy-start.1
  359.0 2.3 copy-start
  359.0 2.3 copy-start.2
  361.3 1.6 copy-start.3
  362.9 2.9 copy-start.5
  362.9 2.9 copy-start.13
  365.7 61.3 %copy-start.14 = (s32[1,1,8]{2,1,0:T(1,128)S(1)}, s32[1,1,8]{2,1,0:T(1,128)}, u32[]{:S(2)}) copy-start(s32[1,1,8]{2,1,0:T(1,128)} %param.16) | copy-start | bytes 100
  366.2 61.6 %collective-permute-start.1 = (bf16[256,1024]{0,1:T(8,128)(2,1)S(1)}, bf16[256,1024]{0,1:T(8,128)(2,1)S(1)}, u32[]{:S(2)}, u32[]{:S(2)}) collective-permute-start(bf16[256,1024]{0,1:T(8,128)(2,1)S(1)} %bitcast.121), channel_id=1, source_target_pairs={{0,1},{1,0},{2,3},{3,2},{4,5},{5,4},{6,7},{7,6},{8,9},{9,8},{10,11... | collective-permute-start | bytes 1572872 | tf_op jit(solution)/shard_map/ppermute | solution.py:38
Sparse Core Ops, SparseCore 0:
  201.8 52.5 all-gather.6
  256.6 49.0 all-gather.4
where the time goes:
time: 437 us; the launch traced here: 436 us
  other arithmetic  168 us (38%)
  waiting for transfers between devices  94.5 us (22%)
  matrix products  61.9 us (14%)
  blocking collectives  58.9 us (13%)
  local copies, waits for them, and re-layouts  33 us (8%)
  between operations  14.4 us (3%)
  starting transfers between devices  4.72 us (1%)
    another operation x4, other arithmetic, on_device(): jax.scipy.linalg.solve_triangular(system, rhs, lower=True, unit_diagonal=...  159 us
    all_gather x2, waiting for transfers between devices, entering(): lax.all_gather(part.astype(kind), axis)  94.5 us
    psum x1, blocking collectives, on_device(): summed = lax.psum(pooled.astype(jnp.bfloat16), 'ctx').astype(jnp.float32)  58.9 us
    dot_general x16, matrix products, combine(): jnp.einsum('hij,hjk->hik', later[0], earlier[1], precision=hi) + later[1]  36.7 us
    while x16, local copies, waits for them, and re-layouts  16.7 us
  transfers between devices with their start and end apart: 4, of which 2 were waited for; matrix products, arithmetic and copies ran while one was open for 4% of the time, Pallas kernels for 0%

commit v1 on v0

v1 whole, which is shorter than its diff:
```python
import functools

import jax
import jax.numpy as jnp
from jax import lax
from jax.experimental import pallas as pl
from jax.experimental.pallas import tpu as pltpu
from jax.sharding import PartitionSpec as P

F32, BF16 = jnp.float32, jnp.bfloat16
HIGHEST = lax.Precision.HIGHEST
NEG = -1e30
SUB = 128
META = 16

NN = (((1,), (0,)), ((), ()))
NT = (((1,), (1,)), ((), ()))
TN = (((0,), (0,)), ((), ()))


def dot(a, b, dims=NN, precision=None):
    return lax.dot_general(a, b, dims, precision=precision, preferred_element_type=F32)


def dot1(a, b, dims=NN):
    return dot(a.astype(BF16), b.astype(BF16), dims)


def split(x):
    high = x.astype(BF16)
    return high, (x - high.astype(F32)).astype(BF16)


def dot3(a, b, dims=NN):
    (ah, al), (bh, bl) = split(a), split(b)
    return dot(ah, bh, dims) + (dot(al, bh, dims) + dot(ah, bl, dims))


def unit(x):
    return x * lax.rsqrt(jnp.sum(x * x, axis=-1, keepdims=True) + 1e-06)


def iotas():
    shape = (SUB, SUB)
    return lax.broadcasted_iota(jnp.int32, shape, 0), lax.broadcasted_iota(jnp.int32, shape, 1)


def per_token(rows, heads, subs):
    return jnp.concatenate([rows[:, j * SUB : (j + 1) * SUB] for j in range(subs)], axis=0)


class Decay:
    def __init__(self, gates, ids, heads, subs):
        r, c = iotas()
        upto = (c <= r).astype(F32)
        logs = per_token(jnp.log(gates), heads, subs)
        self.row = dot(logs, upto, NT, HIGHEST)
        self.col = dot(upto, logs, NT, HIGHEST)
        ids = ids.astype(F32)
        eye = (r == c).astype(F32)
        self.id_row = [ids[:, j * SUB : (j + 1) * SUB] for j in range(subs)]
        stacked = jnp.concatenate([jnp.broadcast_to(x, (8, SUB)) for x in self.id_row], axis=0)
        turned = dot1(eye, stacked, NT)
        self.id_col = [turned[:, 8 * j : 8 * j + 1] for j in range(subs)]
        self.heads, self.r, self.c, self.eye = heads, r, c, eye

    def rows(self, h, j):
        i = j * self.heads + h
        return self.row[i : i + 1, :]

    def cols(self, h, j):
        i = j * self.heads + h
        return self.col[:, i : i + 1]

    def inner(self, h, j):
        keep = (self.id_col[j] == self.id_row[j]) & (self.r >= self.c)
        return jnp.exp(jnp.where(keep, self.cols(h, j) - self.rows(h, j), NEG))

    def entry(self, j):
        return self.id_row[0][:, :1] if j == 0 else self.id_row[j - 1][:, SUB - 1 :]

    def lead(self, h, j):
        return jnp.where(self.id_col[j] == self.entry(j), jnp.exp(self.cols(h, j)), 0.0)

    def lead_end(self, h, j):
        last = self.rows(h, j)[:, SUB - 1 :]
        return jnp.where(self.id_row[j][:, SUB - 1 :] == self.entry(j), jnp.exp(last), 0.0)

    def tail(self, h, j):
        keep = self.id_col[j] == self.id_row[j][:, SUB - 1 :]
        return jnp.exp(jnp.where(keep, self.rows(h, j)[:, SUB - 1 :] - self.cols(h, j), NEG))


def block(ref, h, j):
    return ref[j * SUB : (j + 1) * SUB, h * SUB : (h + 1) * SUB]


def chunk_kernel(
    heads, subs, core_ref, k_ref, v_ref, beta_ref, gates_ref, ids_ref,
    send_ref, keep_ref, wv_ref, yy_ref, p0_ref, u0_ref,
):
    decay = Decay(gates_ref[...], ids_ref[...], heads, subs)
    r, c, eye = decay.r, decay.c, decay.eye
    beta = dot(eye, per_token(beta_ref[...], heads, subs), NT, HIGHEST)
    chains = [(h, j) for j in range(subs) for h in range(heads)]
    kn, low, inv, bt = {}, {}, {}, {}
    for h, j in chains:
        i = j * heads + h
        kn[h, j] = unit(block(k_ref, h, j).astype(F32))
        bt[h, j] = beta[:, i : i + 1]
    for h, j in chains:
        gram = dot1(kn[h, j], kn[h, j], NT)
        full = jnp.where(r > c, bt[h, j] * decay.inner(h, j) * gram, 0.0)
        near = ((r // 2) == (c // 2)) & (r > c)
        inv[h, j] = eye - jnp.where(near, full, 0.0)
        low[h, j] = full.astype(BF16)
    size = 2
    while size < SUB:
        pick = (((r // size) % 2 == 1) & ((c // size) == (r // size) - 1)).astype(BF16)
        half = {}
        for key in chains:
            half[key] = dot1(inv[key], low[key] * pick)
        for key in chains:
            inv[key] = inv[key] - dot1(half[key], inv[key])
        size *= 2
    wv, yy, pp, uu = {}, {}, {}, {}
    for h, j in chains:
        lead = bt[h, j] * decay.lead(h, j)
        xh, xl = split(inv[h, j])
        rh, rl = split(bt[h, j] * block(v_ref, h, j).astype(F32))
        wv[h, j] = dot(xh, rh) + (dot(xl, rh) + dot(xh, rl))
        yy[h, j] = dot(xh, (lead * kn[h, j]).astype(BF16)).astype(BF16)
        wv_ref[j * SUB : (j + 1) * SUB, h * SUB : (h + 1) * SUB] = wv[h, j]
        yy_ref[j * SUB : (j + 1) * SUB, h * SUB : (h + 1) * SUB] = yy[h, j]
    for h, j in chains:
        dh, dl = split(decay.tail(h, j) * kn[h, j])
        wh, wl = split(wv[h, j])
        pp[h, j] = decay.lead_end(h, j) * eye - dot(dh, yy[h, j], TN)
        uu[h, j] = dot(dh, wh, TN) + (dot(dl, wh, TN) + dot(dh, wl, TN))
    for h in range(heads):
        p0_ref[h * SUB : (h + 1) * SUB, :] = pp[h, 0].astype(BF16)
        u0_ref[h * SUB : (h + 1) * SUB, :] = uu[h, 0].astype(BF16)
    for j in range(1, subs):
        for h in range(heads):
            step = pp[h, j].astype(BF16)
            uu[h, 0] = uu[h, j] + dot1(step, uu[h, 0])
            pp[h, 0] = dot1(step, pp[h, 0])
    half_heads = heads // 2
    first = core_ref[0] == 0
    for h in range(half_heads):
        for base, part in ((0, pp), (half_heads, uu)):
            lo, hi = part[h, 0].astype(BF16), part[half_heads + h, 0].astype(BF16)
            at = slice((base + h) * SUB, (base + h + 1) * SUB)
            send_ref[at, :] = jnp.where(first, hi, lo)
            keep_ref[at, :] = jnp.where(first, lo, hi)
    start = decay.id_row[0][:, :1]
    end = decay.id_row[-1][:, SUB - 1 :]
    which = lax.broadcasted_iota(jnp.int32, (META, SUB), 0) < META // 2
    meta = jnp.where(which, end, start).astype(BF16)
    send_ref[heads * SUB :, :] = meta
    keep_ref[heads * SUB :, :] = meta


def query_kernel(
    heads, subs, q_ref, k_ref, gates_ref, ids_ref, wv_ref, yy_ref, p0_ref, u0_ref, local_ref, reach_ref
):
    decay = Decay(gates_ref[...], ids_ref[...], heads, subs)
    chains = [(h, j) for j in range(subs) for h in range(heads)]
    qn, attend, reach, local = {}, {}, {}, {}
    for h, j in chains:
        qn[h, j] = unit(block(q_ref, h, j).astype(F32))
        kn = unit(block(k_ref, h, j).astype(F32))
        attend[h, j] = decay.inner(h, j) * dot3(qn[h, j], kn, NT)
    for h, j in chains:
        ah, al = split(attend[h, j])
        wh, wl = split(block(wv_ref, h, j))
        reach[h, j] = decay.lead(h, j) * qn[h, j] - dot(ah, block(yy_ref, h, j))
        local[h, j] = dot(ah, wh) + (dot(al, wh) + dot(ah, wl))
    for h, j in chains:
        if j > 0:
            rb = reach[h, j].astype(BF16)
            at = slice(h * SUB, (h + 1) * SUB)
            local[h, j] = local[h, j] + dot(rb, u0_ref[at, :])
            reach[h, j] = dot(rb, p0_ref[at, :])
        local_ref[j * SUB : (j + 1) * SUB, h * SUB : (h + 1) * SUB] = local[h, j]
        reach_ref[j * SUB : (j + 1) * SUB, h * SUB : (h + 1) * SUB] = reach[h, j].astype(BF16)


def ends(ref, rows):
    meta = ref[rows : rows + META, :].astype(F32)
    return meta[META // 2 : META // 2 + 1, :], meta[:1, :]


def pair_kernel(heads, core_ref, keep_ref, got_ref, full_ref, tail_ref):
    half = heads // 2
    first = core_ref[0] == 0
    own, other = ends(keep_ref, heads * SUB), ends(got_ref, heads * SUB)
    early = [jnp.where(first, a, b) for a, b in zip(own, other)]
    late = [jnp.where(first, b, a) for a, b in zip(own, other)]
    joined = (early[1] == late[0]).astype(F32)
    for h in range(half):
        at, up = slice(h * SUB, (h + 1) * SUB), slice((half + h) * SUB, (half + h + 1) * SUB)
        p1 = jnp.where(first, keep_ref[at, :], got_ref[at, :])
        p2 = jnp.where(first, got_ref[at, :], keep_ref[at, :])
        u1 = jnp.where(first, keep_ref[up, :], got_ref[up, :])
        u2 = jnp.where(first, got_ref[up, :], keep_ref[up, :])
        full_ref[at, :] = (joined * dot(p2, p1)).astype(BF16)
        state = (u2.astype(F32) + joined * dot(p2, u1)).astype(BF16)
        full_ref[up, :] = state
        tail_ref[at, :] = state
    which = lax.broadcasted_iota(jnp.int32, (META, SUB), 0) < META // 2
    meta = jnp.where(which, late[1], early[0]).astype(BF16)
    full_ref[heads * SUB :, :] = meta
    tail_ref[half * SUB :, :] = meta


def enter_kernel(heads, reach, core_ref, keep_ref, got_ref, *refs):
    chips, (send_ref, mine_ref) = refs[:reach], refs[reach:]
    half = heads // 2
    first = core_ref[0] == 0
    own, other = ends(keep_ref, heads * SUB), ends(got_ref, heads * SUB)
    early = [jnp.where(first, a, b) for a, b in zip(own, other)]
    late = [jnp.where(first, b, a) for a, b in zip(own, other)]
    marks = [(early[0], None)]
    for d, ref in enumerate(chips):
        marks.append(ends(ref, (heads if d < reach - 1 else half) * SUB))
    links = [(marks[d][0] == marks[d + 1][1]).astype(F32) for d in range(reach)]
    joined = (early[1] == late[0]).astype(F32)
    for h in range(half):
        at, up = slice(h * SUB, (h + 1) * SUB), slice((half + h) * SUB, (half + h + 1) * SUB)
        state = chips[-1][at, :].astype(F32)
        for d in range(reach - 2, -1, -1):
            state = chips[d][up, :].astype(F32) + links[d + 1] * dot1(chips[d][at, :], state)
        state = (links[0] * state).astype(BF16)
        p1 = jnp.where(first, keep_ref[at, :], got_ref[at, :])
        u1 = jnp.where(first, keep_ref[up, :], got_ref[up, :])
        middle = (joined * (u1.astype(F32) + dot(p1, state))).astype(BF16)
        send_ref[at, :] = jnp.where(first, middle, state)
        mine_ref[at, :] = jnp.where(first, state, middle)


def rows_kernel(
    heads, ndoc, copies, core_ref, mine_ref, got_ref, local_ref, reach_ref, v_ref, gain_ref, ids_ref,
    out_ref, pooled_ref,
):
    half = heads // 2
    first = core_ref[0] == 0
    length = v_ref.shape[0]
    docs = lax.broadcasted_iota(jnp.int32, (ndoc, length), 0)
    onehot = (docs == ids_ref[...]).astype(F32).astype(BF16)
    gain = gain_ref[...]
    for h in range(heads):
        at = slice((h % half) * SUB, (h % half + 1) * SUB)
        near, far = (mine_ref, got_ref) if h < half else (got_ref, mine_ref)
        state = jnp.where(first, near[at, :], far[at, :])
        cols = slice(h * SUB, (h + 1) * SUB)
        o = local_ref[:, cols] + dot(reach_ref[:, cols], state)
        scale = lax.rsqrt(jnp.sum(o * o, axis=-1, keepdims=True) * (1.0 / SUB) + 1e-06)
        out = (v_ref[:, cols].astype(F32) + o * scale * gain).astype(BF16)
        out_ref[:, cols] = out
        pooled = dot(onehot, out).astype(BF16)
        for i in range(copies):
            pooled_ref[i, :, cols] = pooled


def score(emb, cands, own, pos):
    scores = dot(cands, emb, NT, HIGHEST) / 0.05
    cidx = lax.broadcasted_iota(jnp.int32, scores.shape, 0)
    didx = lax.broadcasted_iota(jnp.int32, scores.shape, 1)
    total = jnp.sum(jnp.where(cidx != own + didx, jnp.exp(scores), 0.0), axis=0, keepdims=True)
    picked = jnp.sum(jnp.where(cidx == pos, scores, 0.0), axis=0, keepdims=True)
    return jnp.log(total) - picked


def loss_kernel(parts_ref, pos_ref, loss_ref):
    emb = unit(jnp.sum(parts_ref[...].astype(F32), axis=0))
    loss_ref[...] = score(emb, emb, 0, pos_ref[...])


def call(body, outs, name, flops=0, scalars=0, n_in=0):
    vmem = pl.BlockSpec(memory_space=pltpu.VMEM)
    smem = pl.BlockSpec(memory_space=pltpu.SMEM)
    return pl.pallas_call(
        body,
        out_shape=[jax.ShapeDtypeStruct(s, d) for s, d in outs],
        in_specs=[smem] * scalars + [vmem] * n_in,
        out_specs=[vmem] * len(outs),
        compiler_params=pltpu.CompilerParams(vmem_limit_bytes=40 << 20),
        cost_estimate=pl.CostEstimate(flops=flops, bytes_accessed=4 << 20, transcendentals=0),
        name=name,
    )


def on_device(rows_in, queries, keys, strengths, gates, doc_ids, positives, norm_gain):
    length, width = rows_in.shape[2], rows_in.shape[3]
    heads, ndoc = strengths.shape[2], positives.shape[2]
    subs = length // SUB
    half = heads // 2
    size, pipes, replicas = (lax.axis_size(x) for x in ("ctx", "pipe", "dp"))
    chips = size // 2
    reach = chips // 4
    v, q, k = rows_in[0, 0], queries[0, 0], keys[0, 0]
    beta, gate, ids = strengths[0, 0], gates[0, 0], doc_ids[0]
    core = (lax.axis_index("ctx") % 2).astype(jnp.int32).reshape(1)

    def swapped(x):
        return lax.ppermute(x, "ctx", [(i, i ^ 1) for i in range(size)])

    def from_behind(x, d):
        return lax.ppermute(x, "ctx", [(i, i + 2 * d) for i in range(size - 2 * d)])

    big = (heads * SUB + META, SUB)
    send, keep, wv, yy, p0, u0 = call(
        functools.partial(chunk_kernel, heads, subs),
        [(big, BF16), (big, BF16), ((length, width), F32), ((length, width), BF16)]
        + [((heads * SUB, SUB), BF16)] * 2,
        "chunks", scalars=1, n_in=5, flops=1 << 31,
    )(core, k, v, beta, gate, ids)
    got = swapped(send)
    full, tail = call(
        functools.partial(pair_kernel, heads),
        [(big, BF16), ((half * SUB + META, SUB), BF16)],
        "pair", scalars=1, n_in=2, flops=1 << 25,
    )(core, keep, got)
    arrived = [from_behind(full, d) for d in range(1, reach)] + [from_behind(tail, reach)]
    local, reached = call(
        functools.partial(query_kernel, heads, subs),
        [((length, width), F32), ((length, width), BF16)],
        "queries", n_in=8, flops=1 << 31,
    )(q, k, gate, ids, wv, yy, p0, u0)
    give, mine = call(
        functools.partial(enter_kernel, heads, reach),
        [((half * SUB, SUB), BF16)] * 2,
        "enter", scalars=1, n_in=2 + reach, flops=1 << 25,
    )(core, keep, got, *arrived)
    theirs = swapped(give)
    rows_out, pooled = call(
        functools.partial(rows_kernel, heads, ndoc, size),
        [((length, width), BF16), ((size, ndoc, width), BF16)],
        "rows", scalars=1, n_in=7, flops=1 << 27,
    )(core, mine, theirs, local, reached, v, norm_gain, ids)
    passed = lax.ppermute(rows_out, "pipe", [(i, (i + 1) % pipes) for i in range(pipes)])
    parts = lax.all_to_all(pooled, "ctx", 0, 0)
    pos = positives[0]
    if replicas == 1:
        (loss,) = call(loss_kernel, [((1, ndoc), F32)], "loss", n_in=2)(parts, pos)
    else:
        mine = unit(jnp.sum(parts.astype(F32), axis=0))
        cands = lax.all_gather(mine.astype(BF16), "dp", axis=0, tiled=True).astype(F32)
        loss = score(mine, cands, lax.axis_index("dp") * ndoc, pos)
    return (passed.reshape(1, 1, length, width), loss.reshape(1, 1, ndoc))


def solution(mesh):
    rows = P(("groups", "pipe"), "dp", "ctx", None)
    tokens = P(("groups", "pipe"), "dp", None, "ctx")
    docs = P(("groups", "pipe"), "dp", None)
    in_specs = (
        rows, rows, rows, tokens, tokens, P(("groups", "pipe"), "dp", "ctx"), docs, P("pipe", None)
    )
    return jax.shard_map(
        on_device, mesh=mesh, in_specs=in_specs, out_specs=(rows, docs), check_vma=False
    )
```

time: 437 us -> 52.5 us (0.12)
  other arithmetic: 168 us -> 0 us
  waiting for transfers between devices: 94.5 us -> 4.02 us
  matrix products: 61.9 us -> 0 us
  blocking collectives: 58.9 us -> 19.2 us
  local copies, waits for them, and re-layouts: 33 us -> 4.88 us
  between operations: 14.4 us -> 0.78 us
  Pallas kernels: 0 us -> 12.8 us
  starting transfers between devices: 4.72 us -> 10.5 us
    another operation x8 -> x0, other arithmetic: 160 us -> none  [the longest x4 159 us: on_device(): jax.scipy.linalg.solve_triangular(system, rhs, lower=True, unit_diagonal=...]
    all_gather x2 -> x0, waiting for transfers between devices: 94.5 us -> none  [entering(): lax.all_gather(part.astype(kind), axis)]
    psum x1 -> x0, blocking collectives: 58.9 us -> none  [on_device(): summed = lax.psum(pooled.astype(jnp.bfloat16), 'ctx').astype(jnp.float32)]
    dot_general x25 -> x0, matrix products: 57.7 us -> none  [the longest x16 36.7 us: combine(): jnp.einsum('hij,hjk->hik', later[0], earlier[1], precision=hi) + later[1]]
    all_to_all x0 -> x1, blocking collectives: none -> 19.2 us  [on_device(): parts = lax.all_to_all(pooled, 'ctx', 0, 0)]
    while x16 -> x0, local copies, waits for them, and re-layouts: 16.7 us -> none
    pallas_call x0 -> x6, Pallas kernels: none -> 12.8 us  [the longest x1 6.88 us: on_device(): call(functools.partial(chunk_kernel, heads, subs), [(big, BF16), (big, BF...]
    another operation x11 -> x0, local copies, waits for them, and re-layouts: 8.57 us -> none
  transfers between devices with their start and end apart: 4 -> 5, of which waited for: 2 -> 2; matrix products, arithmetic and copies ran while one was open for 4% -> 0% of each run, Pallas kernels for 0% -> 6%
where the time goes in v1:
time: 52.5 us; the launch traced here: 52.1 us
  blocking collectives  19.2 us (37%)
  Pallas kernels  12.8 us (24%)
  starting transfers between devices  10.5 us (20%)
  local copies, waits for them, and re-layouts  4.88 us (9%)
  waiting for transfers between devices  4.02 us (8%)
  between operations  0.78 us (1%)
    all_to_all x1, blocking collectives, on_device(): parts = lax.all_to_all(pooled, 'ctx', 0, 0)  19.2 us
    ppermute x2, starting transfers between devices, from_behind(): return lax.ppermute(x, 'ctx', [(i, i + 2 * d) for i in range(size - 2 * d)])  8.42 us
    pallas_call x1, Pallas kernels, on_device(): call(functools.partial(chunk_kernel, heads, subs), [(big, BF16), (big, BF...  6.88 us
    unnamed x21, local copies, waits for them, and re-layouts  4.88 us
    ppermute x2, waiting for transfers between devices, from_behind(): return lax.ppermute(x, 'ctx', [(i, i + 2 * d) for i in range(size - 2 * d)])  2.84 us
    pallas_call x1, Pallas kernels, on_device(): call(functools.partial(query_kernel, heads, subs), [((length, width), F32...  2.3 us
    pallas_call x1, Pallas kernels, on_device(): call(functools.partial(rows_kernel, heads, ndoc, size), [((length, width)...  2.18 us
    ppermute x1, starting transfers between devices, on_device(): lax.ppermute(rows_out, 'pipe', [(i, (i + 1) % pipes) for i in range(pipes)])  1.49 us
  transfers between devices with their start and end apart: 5, of which 2 were waited for; matrix products, arithmetic and copies ran while one was open for 0% of the time, Pallas kernels for 6%

profile of v1, /device:TPU:0, one launch (start us, length us, event | category | flops | bytes accessed | tf_op | source)
XLA Modules:
  0.0 52.1 jit_solution(11580090117520631802)
XLA Ops:
  0.6 0.0 copy-start.9
  0.6 0.0 copy-start.8
  0.7 0.0 copy-start.2
  0.7 0.7 %copy-done.9 = f32[1,1,8,256]{3,2,1,0:T(8,128)S(1)} copy-done((f32[1,1,8,256]{3,2,1,0:T(8,128)S(1)}, f32[1,1,8,256]{3,2,1,0:T(8,128)}, u32[]{:S(2)}) %copy-start.9) | copy-done | bytes 8216
  1.3 0.0 copy-done.8
  1.4 0.0 copy-done.2
  1.4 0.0 copy-start
  1.4 1.0 %copy-done = bf16[1,1,256,1024]{3,2,1,0:T(8,128)(2,1)S(1)} copy-done((bf16[1,1,256,1024]{3,2,1,0:T(8,128)(2,1)S(1)}, bf16[1,1,256,1024]{3,2,1,0:T(8,128)(2,1)}, u32[]{:S(2)}) %copy-start) | copy-done | bytes 524312
  2.4 0.0 copy-start.5
  2.4 1.0 %copy-done.5 = bf16[1,1,256,1024]{3,2,1,0:T(8,128)(2,1)S(1)} copy-done((bf16[1,1,256,1024]{3,2,1,0:T(8,128)(2,1)S(1)}, bf16[1,1,256,1024]{3,2,1,0:T(8,128)(2,1)}, u32[]{:S(2)}) %copy-start.5) | copy-done | bytes 524312
  3.4 6.9 %chunks.1 = (bf16[1040,128]{1,0:T(8,128)(2,1)S(1)}, bf16[1040,128]{1,0:T(8,128)(2,1)S(1)}, f32[256,1024]{1,0:T(8,128)S(1)}, bf16[256,1024]{1,0:T(8,128)(2,1)S(1)...) custom-call(s32[1]{0:T(128)} %bitcast.core_ref, bf16[256,1024]{1,0:T(8,128)(2,1)S(1)} %bitcast.16, ...), custom_call_target="tpu_custom_call" | custom-call | flops 2147483648 | bytes 4194304 | tf_op jit(solution)/shard_map/chunks/pallas_call | solution.py:313
  10.3 0.5 %collective-permute-start = (bf16[1040,128]{1,0:T(8,128)(2,1)S(1)}, bf16[1040,128]{1,0:T(8,128)(2,1)S(1)}, u32[]{:S(2)}, u32[]{:S(2)}) collective-permute-start(bf16[1040,128]{1,0:T(8,128)(2,1)S(1)} %get-tuple-element.17), channel_id=1, source_target_pairs={{0,2},{2,0},{4,6},{6,4},{8,10},{10,8},{12,14},{14,12},{16,18},{18,... | collective-permute-start | bytes 798728 | tf_op jit(solution)/shard_map/ppermute | solution.py:307
  10.9 1.2 %collective-permute-done.got_ref = bf16[1040,128]{1,0:T(8,128)(2,1)S(1)} collective-permute-done((bf16[1040,128]{1,0:T(8,128)(2,1)S(1)}, bf16[1040,128]{1,0:T(8,128)(2,1)S(1)}, u32[]{:S(2)}, u32[]{:S(2)}) %collective-permute-start) | collective-permute-done | bytes 266272 | tf_op jit(solution)/shard_map/ppermute | solution.py:307
  12.0 0.0 copy-start.7
  12.0 0.2 pair.1
  12.3 0.0 copy-start.6
  12.3 4.9 %collective-permute-start.1 = (bf16[1040,128]{1,0:T(8,128)(2,1)S(1)}, bf16[1040,128]{1,0:T(8,128)(2,1)S(1)}, u32[]{:S(2)}, u32[]{:S(2)}) collective-permute-start(bf16[1040,128]{1,0:T(8,128)(2,1)S(1)} %get-tuple-element.18), channel_id=1, source_target_pairs={{0,4},{2,6},{4,8},{6,10},{8,12},{10,14},{12,16},{14,18},{16,20},{1... | collective-permute-start | bytes 798728 | tf_op jit(solution)/shard_map/ppermute | solution.py:310
  17.2 3.5 %collective-permute-start.2 = (bf16[528,128]{1,0:T(8,128)(2,1)S(1)}, bf16[528,128]{1,0:T(8,128)(2,1)S(1)}, u32[]{:S(2)}, u32[]{:S(2)}) collective-permute-start(bf16[528,128]{1,0:T(8,128)(2,1)S(1)} %get-tuple-element.19), channel_id=1, source_target_pairs={{0,8},{2,10},{4,12},{6,14},{8,16},{10,18},{12,20},{14,22},{16,24},... | collective-permute-start | bytes 405512 | tf_op jit(solution)/shard_map/ppermute | solution.py:310
  20.7 2.8 %collective-permute-done.2.refs_1_ = bf16[528,128]{1,0:T(8,128)(2,1)S(1)} collective-permute-done((bf16[528,128]{1,0:T(8,128)(2,1)S(1)}, bf16[528,128]{1,0:T(8,128)(2,1)S(1)}, u32[]{:S(2)}, u32[]{:S(2)}) %collective-permute-start.2) | collective-permute-done | bytes 135200 | tf_op jit(solution)/shard_map/ppermute | solution.py:310
  23.5 0.0 collective-permute-done.1.refs_0_
  23.5 0.3 enter.1
  23.9 0.1 collective-permute-start.3
  24.0 0.0 copy-done.7
  24.0 0.0 copy-done.6
  24.0 0.0 copy-start.1
  24.0 2.3 %queries.1 = (f32[256,1024]{1,0:T(8,128)S(1)}, bf16[256,1024]{1,0:T(8,128)(2,1)S(1)}) custom-call(bf16[256,1024]{1,0:T(8,128)(2,1)S(1)} %bitcast.18, bf16[256,1024]{1,0:T(8,128)(2,1)S(1)} %bitcast.17, f32[8,256]{1,0:T(8,128)S(1)} %bitcast.21, s32[1,256]{1,0:T(1,128)S(1)} %bitcast.13, f32[256,1024]{1,0:T(8,128)S(1)} %get-tuple-element.22.wv_ref, ...), custom_call_target="tpu_custom_call" | custom-call | flops 2147483648 | bytes 4194304 | tf_op jit(solution)/shard_map/queries/pallas_call | solution.py:326
  26.3 0.0 collective-permute-done.3.got_ref
  26.3 0.0 copy-start.4
  26.3 0.0 copy-done.1
  26.3 0.6 %copy-done.4 = f32[1,128]{1,0:T(1,128)S(1)} copy-done((f32[1,128]{1,0:T(1,128)S(1)}, f32[1,128]{1,0:T(1,128)}, u32[]{:S(2)}) %copy-start.4) | copy-done | bytes 536
  27.0 2.2 %rows.1 = (bf16[256,1024]{1,0:T(8,128)(2,1)S(1)}, bf16[16,8,1024]{2,1,0:T(8,128)(2,1)S(1)}) custom-call(s32[1]{0:T(128)} %bitcast.core_ref, bf16[512,128]{1,0:T(8,128)(2,1)S(1)} %get-tuple-element.20.mine_ref, bf16[512,128]{1,0:T(8,128)(2,1)S(1)} %collective-permute-done.3.got_ref, f32[256,1024]{1,0:T(8,128)S(1)} %get-tuple-element.26.local_ref, ...), custom_call_target="tpu_custom_call" | custom-call | flops 134217728 | bytes 4194304 | tf_op jit(solution)/shard_map/rows/pallas_call | solution.py:337
  29.2 1.5 %collective-permute-start.4 = (bf16[256,1024]{1,0:T(8,128)(2,1)S(1)}, bf16[256,1024]{1,0:T(8,128)(2,1)S(1)}, u32[]{:S(2)}, u32[]{:S(2)}) collective-permute-start(bf16[256,1024]{1,0:T(8,128)(2,1)S(1)} %get-tuple-element.28), channel_id=1, source_target_pairs={{0,1},{1,0},{2,3},{3,2},{4,5},{5,4},{6,7},{7,6},{8,9},{9,8},{10,11... | collective-permute-start | bytes 1572872 | tf_op jit(solution)/shard_map/ppermute | solution.py:342
  30.6 19.2 %all_to_all.5.parts_ref = bf16[16,8,1024]{2,1,0:T(8,128)(2,1)S(1)} all-to-all(bf16[16,8,1024]{2,1,0:T(8,128)(2,1)S(1)} %get-tuple-element.29), channel_id=1, replica_groups=mesh['groups'=1,'ctx'=16,'pipe'=2,'dp'=1] {'ctx'}, dimensions={0} | all-to-all | bytes 524288 | tf_op jit(solution)/shard_map/all_to_all | solution.py:343
  49.8 0.0 copy-start.3
  49.8 0.7 %copy-done.3 = s32[1,1,8]{2,1,0:T(1,128)S(1)} copy-done((s32[1,1,8]{2,1,0:T(1,128)S(1)}, s32[1,1,8]{2,1,0:T(1,128)}, u32[]{:S(2)}) %copy-start.3) | copy-done | bytes 56
  50.5 0.8 %loss.1 = f32[1,8]{1,0:T(1,128)} custom-call(bf16[16,8,1024]{2,1,0:T(8,128)(2,1)S(1)} %all_to_all.5.parts_ref, s32[1,8]{1,0:T(1,128)S(1)} %bitcast.15), custom_call_target="tpu_custom_call" | custom-call | bytes 4194304 | tf_op jit(solution)/shard_map/loss/pallas_call | solution.py:346
  51.3 0.0 collective-permute-done.4
  51.3 0.8 %copy.11 = bf16[1,1,256,1024]{3,2,1,0:T(8,128)(2,1)} copy(bf16[1,1,256,1024]{3,2,1,0:T(8,128)(2,1)S(1)} %bitcast.22) | data formatting | bytes 1048576
Async XLA Ops:
  0.6 0.7 %copy-start.9 = (f32[1,1,8,256]{3,2,1,0:T(8,128)S(1)}, f32[1,1,8,256]{3,2,1,0:T(8,128)}, u32[]{:S(2)}) copy-start(f32[1,1,8,256]{3,2,1,0:T(8,128)} %param.12) | copy-start | bytes 24580
  0.6 0.7 %copy-start.8 = (f32[1,1,8,256]{3,2,1,0:T(8,128)S(1)}, f32[1,1,8,256]{3,2,1,0:T(8,128)}, u32[]{:S(2)}) copy-start(f32[1,1,8,256]{3,2,1,0:T(8,128)} %param.11) | copy-start | bytes 24580
  0.7 0.7 %copy-start.2 = (s32[1,1,256]{2,1,0:T(1,128)S(1)}, s32[1,1,256]{2,1,0:T(1,128)}, u32[]{:S(2)}) copy-start(s32[1,1,256]{2,1,0:T(1,128)} %param.13) | copy-start | bytes 3076
  1.4 1.0 %copy-start = (bf16[1,1,256,1024]{3,2,1,0:T(8,128)(2,1)S(1)}, bf16[1,1,256,1024]{3,2,1,0:T(8,128)(2,1)}, u32[]{:S(2)}) copy-start(bf16[1,1,256,1024]{3,2,1,0:T(8,128)(2,1)} %param.8) | copy-start | bytes 1572868
  2.4 1.0 %copy-start.5 = (bf16[1,1,256,1024]{3,2,1,0:T(8,128)(2,1)S(1)}, bf16[1,1,256,1024]{3,2,1,0:T(8,128)(2,1)}, u32[]{:S(2)}) copy-start(bf16[1,1,256,1024]{3,2,1,0:T(8,128)(2,1)} %param.10) | copy-start | bytes 1572868
  10.3 1.7 %collective-permute-start = (bf16[1040,128]{1,0:T(8,128)(2,1)S(1)}, bf16[1040,128]{1,0:T(8,128)(2,1)S(1)}, u32[]{:S(2)}, u32[]{:S(2)}) collective-permute-start(bf16[1040,128]{1,0:T(8,128)(2,1)S(1)} %get-tuple-element.17), channel_id=1, source_target_pairs={{0,2},{2,0},{4,6},{6,4},{8,10},{10,8},{12,14},{14,12},{16,18},{18,... | collective-permute-start | bytes 798728 | tf_op jit(solution)/shard_map/ppermute | solution.py:307
  12.0 12.0 %copy-start.7 = (bf16[1,1,256,1024]{3,2,1,0:T(8,128)(2,1)S(1)}, bf16[1,1,256,1024]{3,2,1,0:T(8,128)(2,1)}, u32[]{:S(2)}) copy-start(bf16[1,1,256,1024]{3,2,1,0:T(8,128)(2,1)} %param.9) | copy-start | bytes 1572868
  12.3 11.7 %copy-start.6 = (bf16[1,1,256,1024]{3,2,1,0:T(8,128)(2,1)S(1)}, bf16[1,1,256,1024]{3,2,1,0:T(8,128)(2,1)}, u32[]{:S(2)}) copy-start(bf16[1,1,256,1024]{3,2,1,0:T(8,128)(2,1)} %param.10) | copy-start | bytes 1572868
  12.3 11.3 %collective-permute-start.1 = (bf16[1040,128]{1,0:T(8,128)(2,1)S(1)}, bf16[1040,128]{1,0:T(8,128)(2,1)S(1)}, u32[]{:S(2)}, u32[]{:S(2)}) collective-permute-start(bf16[1040,128]{1,0:T(8,128)(2,1)S(1)} %get-tuple-element.18), channel_id=1, source_target_pairs={{0,4},{2,6},{4,8},{6,10},{8,12},{10,14},{12,16},{14,18},{16,20},{1... | collective-permute-start | bytes 798728 | tf_op jit(solution)/shard_map/ppermute | solution.py:310
  17.2 6.3 %collective-permute-start.2 = (bf16[528,128]{1,0:T(8,128)(2,1)S(1)}, bf16[528,128]{1,0:T(8,128)(2,1)S(1)}, u32[]{:S(2)}, u32[]{:S(2)}) collective-permute-start(bf16[528,128]{1,0:T(8,128)(2,1)S(1)} %get-tuple-element.19), channel_id=1, source_target_pairs={{0,8},{2,10},{4,12},{6,14},{8,16},{10,18},{12,20},{14,22},{16,24},... | collective-permute-start | bytes 405512 | tf_op jit(solution)/shard_map/ppermute | solution.py:310
  23.9 2.4 %collective-permute-start.3 = (bf16[512,128]{1,0:T(8,128)(2,1)S(1)}, bf16[512,128]{1,0:T(8,128)(2,1)S(1)}, u32[]{:S(2)}, u32[]{:S(2)}) collective-permute-start(bf16[512,128]{1,0:T(8,128)(2,1)S(1)} %get-tuple-element.21), channel_id=1, source_target_pairs={{0,2},{2,0},{4,6},{6,4},{8,10},{10,8},{12,14},{14,12},{16,18},{18,... | collective-permute-start | bytes 393224 | tf_op jit(solution)/shard_map/ppermute | solution.py:307
  24.0 2.3 %copy-start.1 = (bf16[1,1,256,1024]{3,2,1,0:T(8,128)(2,1)S(1)}, bf16[1,1,256,1024]{3,2,1,0:T(8,128)(2,1)}, u32[]{:S(2)}) copy-start(bf16[1,1,256,1024]{3,2,1,0:T(8,128)(2,1)} %param.8) | copy-start | bytes 1572868
  26.3 0.7 %copy-start.4 = (f32[1,128]{1,0:T(1,128)S(1)}, f32[1,128]{1,0:T(1,128)}, u32[]{:S(2)}) copy-start(f32[1,128]{1,0:T(1,128)} %gain_ref.1) | copy-start | bytes 1540
  29.2 22.2 %collective-permute-start.4 = (bf16[256,1024]{1,0:T(8,128)(2,1)S(1)}, bf16[256,1024]{1,0:T(8,128)(2,1)S(1)}, u32[]{:S(2)}, u32[]{:S(2)}) collective-permute-start(bf16[256,1024]{1,0:T(8,128)(2,1)S(1)} %get-tuple-element.28), channel_id=1, source_target_pairs={{0,1},{1,0},{2,3},{3,2},{4,5},{5,4},{6,7},{7,6},{8,9},{9,8},{10,11... | collective-permute-start | bytes 1572872 | tf_op jit(solution)/shard_map/ppermute | solution.py:342
  49.8 0.7 %copy-start.3 = (s32[1,1,8]{2,1,0:T(1,128)S(1)}, s32[1,1,8]{2,1,0:T(1,128)}, u32[]{:S(2)}) copy-start(s32[1,1,8]{2,1,0:T(1,128)} %param.14) | copy-start | bytes 100

commit v2 on v1

--- a/solution.py
+++ b/solution.py
@@ -96,47 +96,72 @@
 
 
 def chunk_kernel(
-    heads, subs, core_ref, k_ref, v_ref, beta_ref, gates_ref, ids_ref,
-    send_ref, keep_ref, wv_ref, yy_ref, p0_ref, u0_ref,
+    heads, subs, core_ref, k_hbm, v_hbm, beta_hbm, gates_hbm, ids_hbm,
+    send_ref, keep_ref, wv_ref, yy_ref, p0_ref, u0_ref, k_ref, v_ref, gates_ref, ids_ref,
+    beta_ref, sems,
 ):
+    small = [(gates_hbm, gates_ref), (ids_hbm, ids_ref), (beta_hbm, beta_ref)]
+    parts = [pl.ds(j * SUB, SUB) for j in range(subs)]
+    large = [(x.at[p, :], y.at[p, :]) for x, y in ((k_hbm, k_ref), (v_hbm, v_ref)) for p in parts]
+    copies = [pltpu.make_async_copy(x, y, sems.at[i]) for i, (x, y) in enumerate(small + large)]
+    for copy in copies:
+        copy.start()
+    for copy in copies[:3]:
+        copy.wait()
     decay = Decay(gates_ref[...], ids_ref[...], heads, subs)
     r, c, eye = decay.r, decay.c, decay.eye
-    beta = dot(eye, per_token(beta_ref[...], heads, subs), NT, HIGHEST)
+    brow = per_token(beta_ref[...], heads, subs)
+    beta = dot(eye, brow, NT, HIGHEST)
     chains = [(h, j) for j in range(subs) for h in range(heads)]
-    kn, low, inv, bt = {}, {}, {}, {}
+    kn, low, inv = {}, {}, {}
+    for h, j in chains:
+        if h == 0:
+            copies[3 + j].wait()
+        kn[h, j] = unit(block(k_ref, h, j).astype(F32))
+    near = ((r // 2) == (c // 2)) & (r > c)
     for h, j in chains:
         i = j * heads + h
-        kn[h, j] = unit(block(k_ref, h, j).astype(F32))
-        bt[h, j] = beta[:, i : i + 1]
-    for h, j in chains:
         gram = dot1(kn[h, j], kn[h, j], NT)
-        full = jnp.where(r > c, bt[h, j] * decay.inner(h, j) * gram, 0.0)
-        near = ((r // 2) == (c // 2)) & (r > c)
+        full = jnp.where(r > c, beta[:, i : i + 1] * decay.inner(h, j) * gram, 0.0)
         inv[h, j] = eye - jnp.where(near, full, 0.0)
         low[h, j] = full.astype(BF16)
     size = 2
     while size < SUB:
         pick = (((r // size) % 2 == 1) & ((c // size) == (r // size) - 1)).astype(BF16)
-        half = {}
+        odd = range(size, SUB, 2 * size)
+        half, rows = {}, {}
         for key in chains:
-            half[key] = dot1(inv[key], low[key] * pick)
+            rows[key] = inv[key]
+            if size >= 8:
+                rows[key] = jnp.concatenate([inv[key][o : o + size] for o in odd], axis=0)
+            half[key] = dot1(rows[key], low[key] * pick)
         for key in chains:
-            inv[key] = inv[key] - dot1(half[key], inv[key])
+            new = rows[key] - dot1(half[key], inv[key])
+            if size >= 8:
+                parts = []
+                for n, o in enumerate(odd):
+                    parts += [inv[key][o - size : o], new[n * size : (n + 1) * size]]
+                new = jnp.concatenate(parts, axis=0)
+            inv[key] = new
         size *= 2
+    for copy in copies[3 + subs :]:
+        copy.wait()
     wv, yy, pp, uu = {}, {}, {}, {}
     for h, j in chains:
-        lead = bt[h, j] * decay.lead(h, j)
-        xh, xl = split(inv[h, j])
-        rh, rl = split(bt[h, j] * block(v_ref, h, j).astype(F32))
-        wv[h, j] = dot(xh, rh) + (dot(xl, rh) + dot(xh, rl))
-        yy[h, j] = dot(xh, (lead * kn[h, j]).astype(BF16)).astype(BF16)
+        i = j * heads + h
+        xh, xl = split(inv[h, j] * brow[i : i + 1, :])
+        both = jnp.concatenate([block(v_ref, h, j), (decay.lead(h, j) * kn[h, j]).astype(BF16)], axis=1)
+        got = dot(xh, both)
+        wv[h, j] = got[:, :SUB] + dot(xl, both[:, :SUB])
+        yy[h, j] = got[:, SUB:].astype(BF16)
         wv_ref[j * SUB : (j + 1) * SUB, h * SUB : (h + 1) * SUB] = wv[h, j]
         yy_ref[j * SUB : (j + 1) * SUB, h * SUB : (h + 1) * SUB] = yy[h, j]
     for h, j in chains:
         dh, dl = split(decay.tail(h, j) * kn[h, j])
         wh, wl = split(wv[h, j])
-        pp[h, j] = decay.lead_end(h, j) * eye - dot(dh, yy[h, j], TN)
-        uu[h, j] = dot(dh, wh, TN) + (dot(dl, wh, TN) + dot(dh, wl, TN))
+        got = dot(dh, jnp.concatenate([wh, yy[h, j]], axis=1), TN)
+        pp[h, j] = decay.lead_end(h, j) * eye - got[:, SUB:]
+        uu[h, j] = got[:, :SUB] + (dot(dl, wh, TN) + dot(dh, wl, TN))
     for h in range(heads):
         p0_ref[h * SUB : (h + 1) * SUB, :] = pp[h, 0].astype(BF16)
         u0_ref[h * SUB : (h + 1) * SUB, :] = uu[h, 0].astype(BF16)
@@ -162,8 +187,11 @@
 
 
 def query_kernel(
-    heads, subs, q_ref, k_ref, gates_ref, ids_ref, wv_ref, yy_ref, p0_ref, u0_ref, local_ref, reach_ref
+    heads, subs, q_ref, k_ref, gates_ref, ids_ref, wv_ref, yy_ref, p0_ref, u0_ref,
+    gain_in, pos_in, local_ref, reach_ref, gain_ref, pos_ref,
 ):
+    gain_ref[...] = gain_in[...]
+    pos_ref[...] = pos_in[...]
     decay = Decay(gates_ref[...], ids_ref[...], heads, subs)
     chains = [(h, j) for j in range(subs) for h in range(heads)]
     qn, attend, reach, local = {}, {}, {}, {}
@@ -240,21 +268,17 @@
 
 
 def rows_kernel(
-    heads, ndoc, copies, core_ref, mine_ref, got_ref, local_ref, reach_ref, v_ref, gain_ref, ids_ref,
-    out_ref, pooled_ref,
+    heads, ndoc, copies, own, core_ref, state_ref, local_ref, reach_ref, v_ref, gain_ref, ids_ref, *refs
 ):
+    out_ref, pooled_ref = refs[-2:]
     half = heads // 2
-    first = core_ref[0] == 0
-    length = v_ref.shape[0]
-    docs = lax.broadcasted_iota(jnp.int32, (ndoc, length), 0)
+    group = core_ref[0] if own else 1 - core_ref[0]
+    docs = lax.broadcasted_iota(jnp.int32, (ndoc, v_ref.shape[0]), 0)
     onehot = (docs == ids_ref[...]).astype(F32).astype(BF16)
     gain = gain_ref[...]
-    for h in range(heads):
-        at = slice((h % half) * SUB, (h % half + 1) * SUB)
-        near, far = (mine_ref, got_ref) if h < half else (got_ref, mine_ref)
-        state = jnp.where(first, near[at, :], far[at, :])
-        cols = slice(h * SUB, (h + 1) * SUB)
-        o = local_ref[:, cols] + dot(reach_ref[:, cols], state)
+    for h in range(half):
+        cols = pl.ds(pl.multiple_of((group * half + h) * SUB, SUB), SUB)
+        o = local_ref[:, cols] + dot(reach_ref[:, cols], state_ref[h * SUB : (h + 1) * SUB, :])
         scale = lax.rsqrt(jnp.sum(o * o, axis=-1, keepdims=True) * (1.0 / SUB) + 1e-06)
         out = (v_ref[:, cols].astype(F32) + o * scale * gain).astype(BF16)
         out_ref[:, cols] = out
@@ -277,14 +301,19 @@
     loss_ref[...] = score(emb, emb, 0, pos_ref[...])
 
 
-def call(body, outs, name, flops=0, scalars=0, n_in=0):
-    vmem = pl.BlockSpec(memory_space=pltpu.VMEM)
-    smem = pl.BlockSpec(memory_space=pltpu.SMEM)
+VMEM = pl.BlockSpec(memory_space=pltpu.VMEM)
+SMEM = pl.BlockSpec(memory_space=pltpu.SMEM)
+HBM = pl.BlockSpec(memory_space=pltpu.HBM)
+
+
+def call(body, outs, name, specs, flops=0, scratch=(), aliases={}):
     return pl.pallas_call(
         body,
         out_shape=[jax.ShapeDtypeStruct(s, d) for s, d in outs],
-        in_specs=[smem] * scalars + [vmem] * n_in,
-        out_specs=[vmem] * len(outs),
+        in_specs=specs,
+        out_specs=[VMEM] * len(outs),
+        scratch_shapes=scratch,
+        input_output_aliases=aliases,
         compiler_params=pltpu.CompilerParams(vmem_limit_bytes=40 << 20),
         cost_estimate=pl.CostEstimate(flops=flops, bytes_accessed=4 << 20, transcendentals=0),
         name=name,
@@ -310,40 +339,46 @@
         return lax.ppermute(x, "ctx", [(i, i + 2 * d) for i in range(size - 2 * d)])
 
     big = (heads * SUB + META, SUB)
-    send, keep, wv, yy, p0, u0 = call(
+    send, keep, wv, yy, p0, u0, k, v, gate, ids = call(
         functools.partial(chunk_kernel, heads, subs),
         [(big, BF16), (big, BF16), ((length, width), F32), ((length, width), BF16)]
-        + [((heads * SUB, SUB), BF16)] * 2,
-        "chunks", scalars=1, n_in=5, flops=1 << 31,
-    )(core, k, v, beta, gate, ids)
+        + [((heads * SUB, SUB), BF16)] * 2 + [((length, width), BF16)] * 2
+        + [((heads, length), F32), ((1, length), jnp.int32)],
+        "chunks", [SMEM] + [HBM] * 5, 1 << 31,
+        [pltpu.VMEM((heads, length), F32), pltpu.SemaphoreType.DMA((3 + 2 * subs,))],
+    )(core, *(pltpu.with_memory_space_constraint(x, pltpu.HBM) for x in (k, v, beta, gate, ids)))
     got = swapped(send)
     full, tail = call(
         functools.partial(pair_kernel, heads),
         [(big, BF16), ((half * SUB + META, SUB), BF16)],
-        "pair", scalars=1, n_in=2, flops=1 << 25,
+        "pair", [SMEM, VMEM, VMEM], 1 << 25,
     )(core, keep, got)
     arrived = [from_behind(full, d) for d in range(1, reach)] + [from_behind(tail, reach)]
-    local, reached = call(
+    local, reached, gain, pos = call(
         functools.partial(query_kernel, heads, subs),
-        [((length, width), F32), ((length, width), BF16)],
-        "queries", n_in=8, flops=1 << 31,
-    )(q, k, gate, ids, wv, yy, p0, u0)
+        [((length, width), F32), ((length, width), BF16), (norm_gain.shape, F32), ((1, ndoc), jnp.int32)],
+        "queries", [VMEM] * 10, 1 << 31,
+    )(q, k, gate, ids, wv, yy, p0, u0, norm_gain, positives[0])
+    arrived, local, reached, gain, pos = lax.optimization_barrier((arrived, local, reached, gain, pos))
     give, mine = call(
         functools.partial(enter_kernel, heads, reach),
         [((half * SUB, SUB), BF16)] * 2,
-        "enter", scalars=1, n_in=2 + reach, flops=1 << 25,
+        "enter", [SMEM] + [VMEM] * (2 + reach), 1 << 25,
     )(core, keep, got, *arrived)
     theirs = swapped(give)
+    outs = [((length, width), BF16), ((size, ndoc, width), BF16)]
+    rest = (local, reached, v, gain, ids)
+    begun = call(
+        functools.partial(rows_kernel, heads, ndoc, size, True), outs, "rows_own", [SMEM] + [VMEM] * 6, 1 << 31
+    )(core, mine, *rest)
     rows_out, pooled = call(
-        functools.partial(rows_kernel, heads, ndoc, size),
-        [((length, width), BF16), ((size, ndoc, width), BF16)],
-        "rows", scalars=1, n_in=7, flops=1 << 27,
-    )(core, mine, theirs, local, reached, v, norm_gain, ids)
+        functools.partial(rows_kernel, heads, ndoc, size, False), outs, "rows_other",
+        [SMEM] + [VMEM] * 8, 1 << 26, aliases={7: 0, 8: 1},
+    )(core, theirs, *rest, *begun)
     passed = lax.ppermute(rows_out, "pipe", [(i, (i + 1) % pipes) for i in range(pipes)])
     parts = lax.all_to_all(pooled, "ctx", 0, 0)
-    pos = positives[0]
     if replicas == 1:
-        (loss,) = call(loss_kernel, [((1, ndoc), F32)], "loss", n_in=2)(parts, pos)
+        (loss,) = call(loss_kernel, [((1, ndoc), F32)], "loss", [VMEM, VMEM])(parts, pos)
     else:
         mine = unit(jnp.sum(parts.astype(F32), axis=0))
         cands = lax.all_gather(mine.astype(BF16), "dp", axis=0, tiled=True).astype(F32)

time: 52.5 us -> 48.1 us (0.916)
  local copies, waits for them, and re-layouts: 4.88 us -> 1.45 us
  waiting for transfers between devices: 4.02 us -> 1.35 us
  Pallas kernels: 12.8 us -> 15 us
    unnamed x21 -> x7, local copies, waits for them, and re-layouts: 4.88 us -> 1.45 us
    ppermute x2, waiting for transfers between devices: 2.84 us -> 0.01 us  [from_behind(): return lax.ppermute(x, 'ctx', [(i, i + 2 * d) for i in range(size - 2 * d)])]
    pallas_call x1, Pallas kernels: 6.88 us -> 8.92 us  [on_device(): call(functools.partial(chunk_kernel, heads, subs), [(big, BF16), (big, BF...]
    pallas_call x2 -> x3, Pallas kernels: 3.02 us -> 3.14 us  [the longest x1 1.16 us: on_device(): call(functools.partial(rows_kernel, heads, ndoc, size, True), outs, 'rows...]
  transfers between devices with their start and end apart: 5 -> 5, of which waited for: 2 -> 2; matrix products, arithmetic and copies ran while one was open for 0% -> 0% of each run, Pallas kernels for 6% -> 9%
where the time goes in v2:
time: 48.1 us; the launch traced here: 47.9 us
  blocking collectives  19 us (40%)
  Pallas kernels  15 us (31%)
  starting transfers between devices  10.4 us (22%)
  local copies, waits for them, and re-layouts  1.45 us (3%)
  waiting for transfers between devices  1.35 us (3%)
  between operations  0.74 us (2%)
    all_to_all x1, blocking collectives, on_device(): parts = lax.all_to_all(pooled, 'ctx', 0, 0)  19 us
    pallas_call x1, Pallas kernels, on_device(): call(functools.partial(chunk_kernel, heads, subs), [(big, BF16), (big, BF...  8.92 us
    ppermute x2, starting transfers between devices, from_behind(): return lax.ppermute(x, 'ctx', [(i, i + 2 * d) for i in range(size - 2 * d)])  8.28 us
    pallas_call x1, Pallas kernels, on_device(): call(functools.partial(query_kernel, heads, subs), [((length, width), F32...  2.33 us
    ppermute x1, starting transfers between devices, on_device(): lax.ppermute(rows_out, 'pipe', [(i, (i + 1) % pipes) for i in range(pipes)])  1.51 us
    unnamed x7, local copies, waits for them, and re-layouts  1.45 us
    ppermute x2, waiting for transfers between devices, swapped(): return lax.ppermute(x, 'ctx', [(i, i ^ 1) for i in range(size)])  1.35 us
    pallas_call x1, Pallas kernels, on_device(): call(functools.partial(rows_kernel, heads, ndoc, size, True), outs, 'rows...  1.16 us
  transfers between devices with their start and end apart: 5, of which 2 were waited for; matrix products, arithmetic and copies ran while one was open for 0% of the time, Pallas kernels for 9%

profile of v2, /device:TPU:0, one launch (start us, length us, event | category | flops | bytes accessed | tf_op | source)
XLA Modules:
  0.0 47.9 jit_solution(1136682073301223548)
XLA Ops:
  0.6 8.9 %chunks.1 = (bf16[1040,128]{1,0:T(8,128)(2,1)S(1)}, bf16[1040,128]{1,0:T(8,128)(2,1)S(1)}, f32[256,1024]{1,0:T(8,128)S(1)}, bf16[256,1024]{1,0:T(8,128)(2,1)S(1)...) custom-call(s32[1]{0:T(128)} %bitcast.core_ref, ...), custom_call_target="tpu_custom_call" | custom-call | flops 2147483648 | bytes 4194304 | tf_op jit(solution)/shard_map/chunks/pallas_call | solution.py:342
  9.6 0.0 copy-start
  9.6 0.5 %collective-permute-start = (bf16[1040,128]{1,0:T(8,128)(2,1)S(1)}, bf16[1040,128]{1,0:T(8,128)(2,1)S(1)}, u32[]{:S(2)}, u32[]{:S(2)}) collective-permute-start(bf16[1040,128]{1,0:T(8,128)(2,1)S(1)} %get-tuple-element.31), channel_id=1, source_target_pairs={{0,2},{2,0},{4,6},{6,4},{8,10},{10,8},{12,14},{14,12},{16,18},{18,... | collective-permute-start | bytes 798728 | tf_op jit(solution)/shard_map/ppermute | solution.py:336
  10.1 1.2 %collective-permute-done.got_ref = bf16[1040,128]{1,0:T(8,128)(2,1)S(1)} collective-permute-done((bf16[1040,128]{1,0:T(8,128)(2,1)S(1)}, bf16[1040,128]{1,0:T(8,128)(2,1)S(1)}, u32[]{:S(2)}, u32[]{:S(2)}) %collective-permute-start) | collective-permute-done | bytes 266272 | tf_op jit(solution)/shard_map/ppermute | solution.py:336
  11.3 0.2 pair.1
  11.5 4.8 %collective-permute-start.1 = (bf16[1040,128]{1,0:T(8,128)(2,1)S(1)}, bf16[1040,128]{1,0:T(8,128)(2,1)S(1)}, u32[]{:S(2)}, u32[]{:S(2)}) collective-permute-start(bf16[1040,128]{1,0:T(8,128)(2,1)S(1)} %get-tuple-element.32), channel_id=1, source_target_pairs={{0,4},{2,6},{4,8},{6,10},{8,12},{10,14},{12,16},{14,18},{16,20},{1... | collective-permute-start | bytes 798728 | tf_op jit(solution)/shard_map/ppermute | solution.py:339
  16.3 3.5 %collective-permute-start.2 = (bf16[528,128]{1,0:T(8,128)(2,1)S(1)}, bf16[528,128]{1,0:T(8,128)(2,1)S(1)}, u32[]{:S(2)}, u32[]{:S(2)}) collective-permute-start(bf16[528,128]{1,0:T(8,128)(2,1)S(1)} %get-tuple-element.33), channel_id=1, source_target_pairs={{0,8},{2,10},{4,12},{6,14},{8,16},{10,18},{12,20},{14,22},{16,24},... | collective-permute-start | bytes 405512 | tf_op jit(solution)/shard_map/ppermute | solution.py:339
  19.8 0.0 copy-start.1
  19.8 0.0 copy-start.2
  19.8 0.0 copy-done
  19.8 0.6 %copy-done.1 = f32[1,128]{1,0:T(1,128)S(1)} copy-done((f32[1,128]{1,0:T(1,128)S(1)}, f32[1,128]{1,0:T(1,128)}, u32[]{:S(2)}) %copy-start.1) | copy-done | bytes 536
  20.5 0.0 copy-done.2
  20.5 2.3 %queries.1 = (f32[256,1024]{1,0:T(8,128)S(1)}, bf16[256,1024]{1,0:T(8,128)(2,1)S(1)}, f32[1,128]{1,0:T(1,128)S(1)}, s32[1,8]{1,0:T(1,128)S(1)}) custom-call(bf16[256,1024]{1,0:T(8,128)(2,1)S(1)} %bitcast.10, bf16[256,1024]{1,0:T(8,128)(2,1)S(1)} %get-tuple-element.34.k_ref, f32[8,256]{1,0:T(8,128)S(1)} %get-tuple-element.35.gates_ref, ...), custom_call_target="tpu_custom_call" | custom-call | flops 2147483648 | bytes 4194304 | tf_op jit(solution)/shard_map/queries/pallas_call | solution.py:357
  22.8 0.0 collective-permute-done.2.refs_1_
  22.8 0.0 collective-permute-done.1.refs_0_
  22.8 0.4 enter.1
  23.2 0.1 collective-permute-start.3
  23.3 1.2 %rows_own.1 = (bf16[256,1024]{1,0:T(8,128)(2,1)S(1)}, bf16[16,8,1024]{2,1,0:T(8,128)(2,1)S(1)}) custom-call(s32[1]{0:T(128)} %bitcast.core_ref, bf16[512,128]{1,0:T(8,128)(2,1)S(1)} %get-tuple-element.52.state_ref, f32[256,1024]{1,0:T(8,128)S(1)} %get-tuple-element.48.local_ref, bf16[256,1024]{1,0:T(8,128)(2,1)S(1)} %get-tuple-element.49.reach_ref, ...), custom_call_target="tpu_custom_call" | custom-call | flops 2147483648 | bytes 4194304 | tf_op jit(solution)/shard_map/rows_own/pallas_call | solution.py:371
  24.4 0.2 collective-permute-done.3.state_ref
  24.6 1.1 %rows_other.1 = (bf16[256,1024]{1,0:T(8,128)(2,1)S(1)}, bf16[16,8,1024]{2,1,0:T(8,128)(2,1)S(1)}) custom-call(s32[1]{0:T(128)} %bitcast.core_ref, bf16[512,128]{1,0:T(8,128)(2,1)S(1)} %collective-permute-done.3.state_ref, f32[256,1024]{1,0:T(8,128)S(1)} %get-tuple-element.48.local_ref, ...), custom_call_target="tpu_custom_call", output_to_operand_aliasing={{0}: (7, {}), {1}: (8, {})} | custom-call | flops 67108864 | bytes 4194304 | tf_op jit(solution)/shard_map/rows_other/pallas_call | solution.py:374
  25.8 1.5 %collective-permute-start.4 = (bf16[256,1024]{1,0:T(8,128)(2,1)S(1)}, bf16[256,1024]{1,0:T(8,128)(2,1)S(1)}, u32[]{:S(2)}, u32[]{:S(2)}) collective-permute-start(bf16[256,1024]{1,0:T(8,128)(2,1)S(1)} %get-tuple-element.55), channel_id=1, source_target_pairs={{0,1},{1,0},{2,3},{3,2},{4,5},{5,4},{6,7},{7,6},{8,9},{9,8},{10,11... | collective-permute-start | bytes 1572872 | tf_op jit(solution)/shard_map/ppermute | solution.py:378
  27.3 19.0 %all_to_all.5.parts_ref = bf16[16,8,1024]{2,1,0:T(8,128)(2,1)S(1)} all-to-all(bf16[16,8,1024]{2,1,0:T(8,128)(2,1)S(1)} %get-tuple-element.56), channel_id=1, replica_groups=mesh['groups'=1,'ctx'=16,'pipe'=2,'dp'=1] {'ctx'}, dimensions={0} | all-to-all | bytes 524288 | tf_op jit(solution)/shard_map/all_to_all | solution.py:379
  46.2 0.8 %loss.1 = f32[1,8]{1,0:T(1,128)} custom-call(bf16[16,8,1024]{2,1,0:T(8,128)(2,1)S(1)} %all_to_all.5.parts_ref, s32[1,8]{1,0:T(1,128)S(1)} %get-tuple-element.57.pos_ref), custom_call_target="tpu_custom_call" | custom-call | bytes 4194304 | tf_op jit(solution)/shard_map/loss/pallas_call | solution.py:381
  47.1 0.0 collective-permute-done.4
  47.1 0.8 %copy.15 = bf16[1,1,256,1024]{3,2,1,0:T(8,128)(2,1)} copy(bf16[1,1,256,1024]{3,2,1,0:T(8,128)(2,1)S(1)} %bitcast.12) | data formatting | bytes 1048576
Async XLA Ops:
  9.6 10.3 %copy-start = (bf16[1,1,256,1024]{3,2,1,0:T(8,128)(2,1)S(1)}, bf16[1,1,256,1024]{3,2,1,0:T(8,128)(2,1)}, u32[]{:S(2)}) copy-start(bf16[1,1,256,1024]{3,2,1,0:T(8,128)(2,1)} %param.9) | copy-start | bytes 1572868
  9.6 1.7 %collective-permute-start = (bf16[1040,128]{1,0:T(8,128)(2,1)S(1)}, bf16[1040,128]{1,0:T(8,128)(2,1)S(1)}, u32[]{:S(2)}, u32[]{:S(2)}) collective-permute-start(bf16[1040,128]{1,0:T(8,128)(2,1)S(1)} %get-tuple-element.31), channel_id=1, source_target_pairs={{0,2},{2,0},{4,6},{6,4},{8,10},{10,8},{12,14},{14,12},{16,18},{18,... | collective-permute-start | bytes 798728 | tf_op jit(solution)/shard_map/ppermute | solution.py:336
  11.5 11.3 %collective-permute-start.1 = (bf16[1040,128]{1,0:T(8,128)(2,1)S(1)}, bf16[1040,128]{1,0:T(8,128)(2,1)S(1)}, u32[]{:S(2)}, u32[]{:S(2)}) collective-permute-start(bf16[1040,128]{1,0:T(8,128)(2,1)S(1)} %get-tuple-element.32), channel_id=1, source_target_pairs={{0,4},{2,6},{4,8},{6,10},{8,12},{10,14},{12,16},{14,18},{16,20},{1... | collective-permute-start | bytes 798728 | tf_op jit(solution)/shard_map/ppermute | solution.py:339
  16.3 6.5 %collective-permute-start.2 = (bf16[528,128]{1,0:T(8,128)(2,1)S(1)}, bf16[528,128]{1,0:T(8,128)(2,1)S(1)}, u32[]{:S(2)}, u32[]{:S(2)}) collective-permute-start(bf16[528,128]{1,0:T(8,128)(2,1)S(1)} %get-tuple-element.33), channel_id=1, source_target_pairs={{0,8},{2,10},{4,12},{6,14},{8,16},{10,18},{12,20},{14,22},{16,24},... | collective-permute-start | bytes 405512 | tf_op jit(solution)/shard_map/ppermute | solution.py:339
  19.8 0.7 %copy-start.1 = (f32[1,128]{1,0:T(1,128)S(1)}, f32[1,128]{1,0:T(1,128)}, u32[]{:S(2)}) copy-start(f32[1,128]{1,0:T(1,128)} %gain_in.1) | copy-start | bytes 1540
  19.8 0.7 %copy-start.2 = (s32[1,1,8]{2,1,0:T(1,128)S(1)}, s32[1,1,8]{2,1,0:T(1,128)}, u32[]{:S(2)}) copy-start(s32[1,1,8]{2,1,0:T(1,128)} %param.14) | copy-start | bytes 100
  23.2 1.4 %collective-permute-start.3 = (bf16[512,128]{1,0:T(8,128)(2,1)S(1)}, bf16[512,128]{1,0:T(8,128)(2,1)S(1)}, u32[]{:S(2)}, u32[]{:S(2)}) collective-permute-start(bf16[512,128]{1,0:T(8,128)(2,1)S(1)} %get-tuple-element.47), channel_id=1, source_target_pairs={{0,2},{2,0},{4,6},{6,4},{8,10},{10,8},{12,14},{14,12},{16,18},{18,... | collective-permute-start | bytes 393224 | tf_op jit(solution)/shard_map/ppermute | solution.py:336
  25.8 21.3 %collective-permute-start.4 = (bf16[256,1024]{1,0:T(8,128)(2,1)S(1)}, bf16[256,1024]{1,0:T(8,128)(2,1)S(1)}, u32[]{:S(2)}, u32[]{:S(2)}) collective-permute-start(bf16[256,1024]{1,0:T(8,128)(2,1)S(1)} %get-tuple-element.55), channel_id=1, source_target_pairs={{0,1},{1,0},{2,3},{3,2},{4,5},{5,4},{6,7},{7,6},{8,9},{9,8},{10,11... | collective-permute-start | bytes 1572872 | tf_op jit(solution)/shard_map/ppermute | solution.py:378

commit v3 on v2

--- a/solution.py
+++ b/solution.py
@@ -57,38 +57,25 @@
         self.row = dot(logs, upto, NT, HIGHEST)
         self.col = dot(upto, logs, NT, HIGHEST)
         ids = ids.astype(F32)
-        eye = (r == c).astype(F32)
+        self.eye = (r == c).astype(F32)
         self.id_row = [ids[:, j * SUB : (j + 1) * SUB] for j in range(subs)]
         stacked = jnp.concatenate([jnp.broadcast_to(x, (8, SUB)) for x in self.id_row], axis=0)
-        turned = dot1(eye, stacked, NT)
+        turned = dot1(self.eye, stacked, NT)
         self.id_col = [turned[:, 8 * j : 8 * j + 1] for j in range(subs)]
-        self.heads, self.r, self.c, self.eye = heads, r, c, eye
-
-    def rows(self, h, j):
+        self.heads, self.r, self.c = heads, r, c
+        lead, tail = [], []
+        for j in range(subs):
+            row, last = self.row[j * heads : (j + 1) * heads], self.id_row[j][:, SUB - 1 :]
+            entry = self.id_row[0][:, :1] if j == 0 else self.id_row[j - 1][:, SUB - 1 :]
+            lead.append(jnp.where(self.id_row[j] == entry, jnp.exp(row), 0.0))
+            tail.append(jnp.exp(jnp.where(self.id_row[j] == last, row[:, SUB - 1 :] - row, NEG)))
+        self.lead = jnp.concatenate(lead, axis=0)
+        self.tail = jnp.concatenate(tail, axis=0)
+        self.same = [(x == y) & (r >= c) for x, y in zip(self.id_col, self.id_row)]
+
+    def inner(self, h, j, keep):
         i = j * self.heads + h
-        return self.row[i : i + 1, :]
-
-    def cols(self, h, j):
-        i = j * self.heads + h
-        return self.col[:, i : i + 1]
-
-    def inner(self, h, j):
-        keep = (self.id_col[j] == self.id_row[j]) & (self.r >= self.c)
-        return jnp.exp(jnp.where(keep, self.cols(h, j) - self.rows(h, j), NEG))
-
-    def entry(self, j):
-        return self.id_row[0][:, :1] if j == 0 else self.id_row[j - 1][:, SUB - 1 :]
-
-    def lead(self, h, j):
-        return jnp.where(self.id_col[j] == self.entry(j), jnp.exp(self.cols(h, j)), 0.0)
-
-    def lead_end(self, h, j):
-        last = self.rows(h, j)[:, SUB - 1 :]
-        return jnp.where(self.id_row[j][:, SUB - 1 :] == self.entry(j), jnp.exp(last), 0.0)
-
-    def tail(self, h, j):
-        keep = self.id_col[j] == self.id_row[j][:, SUB - 1 :]
-        return jnp.exp(jnp.where(keep, self.rows(h, j)[:, SUB - 1 :] - self.cols(h, j), NEG))
+        return jnp.exp(jnp.where(keep[j], self.col[:, i : i + 1] - self.row[i : i + 1, :], NEG))
 
 
 def block(ref, h, j):
@@ -97,8 +84,8 @@
 
 def chunk_kernel(
     heads, subs, core_ref, k_hbm, v_hbm, beta_hbm, gates_hbm, ids_hbm,
-    send_ref, keep_ref, wv_ref, yy_ref, p0_ref, u0_ref, k_ref, v_ref, gates_ref, ids_ref,
-    beta_ref, sems,
+    send_ref, keep_ref, wv_ref, yy_ref, p0_ref, u0_ref, k_ref, v_ref,
+    beta_ref, gates_ref, ids_ref, sems,
 ):
     small = [(gates_hbm, gates_ref), (ids_hbm, ids_ref), (beta_hbm, beta_ref)]
     parts = [pl.ds(j * SUB, SUB) for j in range(subs)]
@@ -110,19 +97,22 @@
         copy.wait()
     decay = Decay(gates_ref[...], ids_ref[...], heads, subs)
     r, c, eye = decay.r, decay.c, decay.eye
-    brow = per_token(beta_ref[...], heads, subs)
-    beta = dot(eye, brow, NT, HIGHEST)
+    beta = per_token(beta_ref[...], heads, subs)
+    tails = decay.tail * beta
+    strict = [x & (r > c) for x in decay.same]
     chains = [(h, j) for j in range(subs) for h in range(heads)]
-    kn, low, inv = {}, {}, {}
+    kn, kt, low, inv = {}, {}, {}, {}
     for h, j in chains:
         if h == 0:
             copies[3 + j].wait()
-        kn[h, j] = unit(block(k_ref, h, j).astype(F32))
+        unit_keys = unit(block(k_ref, h, j).astype(F32))
+        kn[h, j] = unit_keys.astype(BF16)
+        kt[h, j] = unit_keys.T
     near = ((r // 2) == (c // 2)) & (r > c)
     for h, j in chains:
         i = j * heads + h
-        gram = dot1(kn[h, j], kn[h, j], NT)
-        full = jnp.where(r > c, beta[:, i : i + 1] * decay.inner(h, j) * gram, 0.0)
+        gram = dot(kn[h, j], kt[h, j].astype(BF16))
+        full = decay.inner(h, j, strict) * gram * beta[i : i + 1, :]
         inv[h, j] = eye - jnp.where(near, full, 0.0)
         low[h, j] = full.astype(BF16)
     size = 2
@@ -149,27 +139,28 @@
     wv, yy, pp, uu = {}, {}, {}, {}
     for h, j in chains:
         i = j * heads + h
-        xh, xl = split(inv[h, j] * brow[i : i + 1, :])
-        both = jnp.concatenate([block(v_ref, h, j), (decay.lead(h, j) * kn[h, j]).astype(BF16)], axis=1)
-        got = dot(xh, both)
-        wv[h, j] = got[:, :SUB] + dot(xl, both[:, :SUB])
-        yy[h, j] = got[:, SUB:].astype(BF16)
+        xh, xl = split(inv[h, j])
+        values = block(v_ref, h, j)
+        wv[h, j] = dot(xh, values) + dot(xl, values)
+        yy[h, j] = dot((inv[h, j] * decay.lead[i : i + 1, :]).astype(BF16), kn[h, j]).astype(BF16)
         wv_ref[j * SUB : (j + 1) * SUB, h * SUB : (h + 1) * SUB] = wv[h, j]
         yy_ref[j * SUB : (j + 1) * SUB, h * SUB : (h + 1) * SUB] = yy[h, j]
     for h, j in chains:
-        dh, dl = split(decay.tail(h, j) * kn[h, j])
+        i = j * heads + h
+        dh, dl = split(kt[h, j] * tails[i : i + 1, :])
         wh, wl = split(wv[h, j])
-        got = dot(dh, jnp.concatenate([wh, yy[h, j]], axis=1), TN)
-        pp[h, j] = decay.lead_end(h, j) * eye - got[:, SUB:]
-        uu[h, j] = got[:, :SUB] + (dot(dl, wh, TN) + dot(dh, wl, TN))
+        got = dot(dh, jnp.concatenate([wh, yy[h, j]], axis=1))
+        pp[h, j] = decay.lead[i : i + 1, SUB - 1 :] * eye - got[:, SUB:]
+        uu[h, j] = got[:, :SUB] + (dot(dl, wh) + dot(dh, wl))
     for h in range(heads):
-        p0_ref[h * SUB : (h + 1) * SUB, :] = pp[h, 0].astype(BF16)
-        u0_ref[h * SUB : (h + 1) * SUB, :] = uu[h, 0].astype(BF16)
-    for j in range(1, subs):
-        for h in range(heads):
-            step = pp[h, j].astype(BF16)
-            uu[h, 0] = uu[h, j] + dot1(step, uu[h, 0])
-            pp[h, 0] = dot1(step, pp[h, 0])
+        p0, u0 = pp[h, 0].astype(BF16), uu[h, 0].astype(BF16)
+        p0_ref[h * SUB : (h + 1) * SUB, :] = p0
+        u0_ref[h * SUB : (h + 1) * SUB, :] = u0
+        for j in range(1, subs):
+            got = dot1(pp[h, j], jnp.concatenate([u0, p0], axis=1))
+            uu[h, 0] = uu[h, j] + got[:, :SUB]
+            pp[h, 0] = got[:, SUB:]
+            u0, p0 = uu[h, 0].astype(BF16), pp[h, 0].astype(BF16)
     half_heads = heads // 2
     first = core_ref[0] == 0
     for h in range(half_heads):
@@ -187,22 +178,26 @@
 
 
 def query_kernel(
-    heads, subs, q_ref, k_ref, gates_ref, ids_ref, wv_ref, yy_ref, p0_ref, u0_ref,
+    heads, subs, q_ref, k_ref, beta_ref, gates_ref, ids_ref, wv_ref, yy_ref, p0_ref, u0_ref,
     gain_in, pos_in, local_ref, reach_ref, gain_ref, pos_ref,
 ):
     gain_ref[...] = gain_in[...]
     pos_ref[...] = pos_in[...]
     decay = Decay(gates_ref[...], ids_ref[...], heads, subs)
+    beta = per_token(beta_ref[...], heads, subs)
+    lead = dot(decay.eye, decay.lead, NT, HIGHEST)
     chains = [(h, j) for j in range(subs) for h in range(heads)]
     qn, attend, reach, local = {}, {}, {}, {}
     for h, j in chains:
+        i = j * heads + h
         qn[h, j] = unit(block(q_ref, h, j).astype(F32))
         kn = unit(block(k_ref, h, j).astype(F32))
-        attend[h, j] = decay.inner(h, j) * dot3(qn[h, j], kn, NT)
-    for h, j in chains:
+        attend[h, j] = decay.inner(h, j, decay.same) * dot3(qn[h, j], kn, NT) * beta[i : i + 1, :]
+    for h, j in chains:
+        i = j * heads + h
         ah, al = split(attend[h, j])
         wh, wl = split(block(wv_ref, h, j))
-        reach[h, j] = decay.lead(h, j) * qn[h, j] - dot(ah, block(yy_ref, h, j))
+        reach[h, j] = lead[:, i : i + 1] * qn[h, j] - dot(ah, block(yy_ref, h, j))
         local[h, j] = dot(ah, wh) + (dot(al, wh) + dot(ah, wl))
     for h, j in chains:
         if j > 0:
@@ -339,13 +334,13 @@
         return lax.ppermute(x, "ctx", [(i, i + 2 * d) for i in range(size - 2 * d)])
 
     big = (heads * SUB + META, SUB)
-    send, keep, wv, yy, p0, u0, k, v, gate, ids = call(
+    send, keep, wv, yy, p0, u0, k, v, beta, gate, ids = call(
         functools.partial(chunk_kernel, heads, subs),
         [(big, BF16), (big, BF16), ((length, width), F32), ((length, width), BF16)]
         + [((heads * SUB, SUB), BF16)] * 2 + [((length, width), BF16)] * 2
-        + [((heads, length), F32), ((1, length), jnp.int32)],
+        + [((heads, length), F32)] * 2 + [((1, length), jnp.int32)],
         "chunks", [SMEM] + [HBM] * 5, 1 << 31,
-        [pltpu.VMEM((heads, length), F32), pltpu.SemaphoreType.DMA((3 + 2 * subs,))],
+        [pltpu.SemaphoreType.DMA((3 + 2 * subs,))],
     )(core, *(pltpu.with_memory_space_constraint(x, pltpu.HBM) for x in (k, v, beta, gate, ids)))
     got = swapped(send)
     full, tail = call(
@@ -357,8 +352,8 @@
     local, reached, gain, pos = call(
         functools.partial(query_kernel, heads, subs),
         [((length, width), F32), ((length, width), BF16), (norm_gain.shape, F32), ((1, ndoc), jnp.int32)],
-        "queries", [VMEM] * 10, 1 << 31,
-    )(q, k, gate, ids, wv, yy, p0, u0, norm_gain, positives[0])
+        "queries", [VMEM] * 11, 1 << 31,
+    )(q, k, beta, gate, ids, wv, yy, p0, u0, norm_gain, positives[0])
     arrived, local, reached, gain, pos = lax.optimization_barrier((arrived, local, reached, gain, pos))
     give, mine = call(
         functools.partial(enter_kernel, heads, reach),

time: 48.1 us -> 44.8 us (0.931)
  Pallas kernels: 15 us -> 11.8 us
    pallas_call x1, Pallas kernels: 8.92 us -> 5.59 us  [on_device(): call(functools.partial(chunk_kernel, heads, subs), [(big, BF16), (big, BF...]
  transfers between devices with their start and end apart: 5 -> 5, of which waited for: 2 -> 2; matrix products, arithmetic and copies ran while one was open for 0% -> 0% of each run, Pallas kernels for 9% -> 10%
where the time goes in v3:
time: 44.8 us; the launch traced here: 44.5 us
  blocking collectives  18.8 us (42%)
  Pallas kernels  11.8 us (26%)
  starting transfers between devices  10.4 us (23%)
  local copies, waits for them, and re-layouts  1.45 us (3%)
  waiting for transfers between devices  1.36 us (3%)
  between operations  0.75 us (2%)
    all_to_all x1, blocking collectives, on_device(): parts = lax.all_to_all(pooled, 'ctx', 0, 0)  18.8 us
    ppermute x2, starting transfers between devices, from_behind(): return lax.ppermute(x, 'ctx', [(i, i + 2 * d) for i in range(size - 2 * d)])  8.28 us
    pallas_call x1, Pallas kernels, on_device(): call(functools.partial(chunk_kernel, heads, subs), [(big, BF16), (big, BF...  5.59 us
    pallas_call x1, Pallas kernels, on_device(): call(functools.partial(query_kernel, heads, subs), [((length, width), F32...  2.47 us
    ppermute x1, starting transfers between devices, on_device(): lax.ppermute(rows_out, 'pipe', [(i, (i + 1) % pipes) for i in range(pipes)])  1.5 us
    unnamed x7, local copies, waits for them, and re-layouts  1.45 us
    ppermute x2, waiting for transfers between devices, swapped(): return lax.ppermute(x, 'ctx', [(i, i ^ 1) for i in range(size)])  1.35 us
    pallas_call x1, Pallas kernels, on_device(): call(functools.partial(rows_kernel, heads, ndoc, size, True), outs, 'rows...  1.15 us
  transfers between devices with their start and end apart: 5, of which 2 were waited for; matrix products, arithmetic and copies ran while one was open for 0% of the time, Pallas kernels for 10%

profile of v3, /device:TPU:0, one launch (start us, length us, event | category | flops | bytes accessed | tf_op | source)
XLA Modules:
  0.0 44.5 jit_solution(5536639413712471700)
XLA Ops:
  0.6 5.6 %chunks.1 = (bf16[1040,128]{1,0:T(8,128)(2,1)S(1)}, bf16[1040,128]{1,0:T(8,128)(2,1)S(1)}, f32[256,1024]{1,0:T(8,128)S(1)}, bf16[256,1024]{1,0:T(8,128)(2,1)S(1)...) custom-call(s32[1]{0:T(128)} %bitcast.core_ref, ...), custom_call_target="tpu_custom_call" | custom-call | flops 2147483648 | bytes 4194304 | tf_op jit(solution)/shard_map/chunks/pallas_call | solution.py:337
  6.2 0.0 copy-start
  6.2 0.5 %collective-permute-start = (bf16[1040,128]{1,0:T(8,128)(2,1)S(1)}, bf16[1040,128]{1,0:T(8,128)(2,1)S(1)}, u32[]{:S(2)}, u32[]{:S(2)}) collective-permute-start(bf16[1040,128]{1,0:T(8,128)(2,1)S(1)} %get-tuple-element.32), channel_id=1, source_target_pairs={{0,2},{2,0},{4,6},{6,4},{8,10},{10,8},{12,14},{14,12},{16,18},{18,... | collective-permute-start | bytes 798728 | tf_op jit(solution)/shard_map/ppermute | solution.py:331
  6.8 1.2 %collective-permute-done.got_ref = bf16[1040,128]{1,0:T(8,128)(2,1)S(1)} collective-permute-done((bf16[1040,128]{1,0:T(8,128)(2,1)S(1)}, bf16[1040,128]{1,0:T(8,128)(2,1)S(1)}, u32[]{:S(2)}, u32[]{:S(2)}) %collective-permute-start) | collective-permute-done | bytes 266272 | tf_op jit(solution)/shard_map/ppermute | solution.py:331
  7.9 0.2 pair.1
  8.2 4.8 %collective-permute-start.1 = (bf16[1040,128]{1,0:T(8,128)(2,1)S(1)}, bf16[1040,128]{1,0:T(8,128)(2,1)S(1)}, u32[]{:S(2)}, u32[]{:S(2)}) collective-permute-start(bf16[1040,128]{1,0:T(8,128)(2,1)S(1)} %get-tuple-element.33), channel_id=1, source_target_pairs={{0,4},{2,6},{4,8},{6,10},{8,12},{10,14},{12,16},{14,18},{16,20},{1... | collective-permute-start | bytes 798728 | tf_op jit(solution)/shard_map/ppermute | solution.py:334
  13.0 3.5 %collective-permute-start.2 = (bf16[528,128]{1,0:T(8,128)(2,1)S(1)}, bf16[528,128]{1,0:T(8,128)(2,1)S(1)}, u32[]{:S(2)}, u32[]{:S(2)}) collective-permute-start(bf16[528,128]{1,0:T(8,128)(2,1)S(1)} %get-tuple-element.34), channel_id=1, source_target_pairs={{0,8},{2,10},{4,12},{6,14},{8,16},{10,18},{12,20},{14,22},{16,24},... | collective-permute-start | bytes 405512 | tf_op jit(solution)/shard_map/ppermute | solution.py:334
  16.5 0.0 copy-start.1
  16.5 0.0 copy-start.2
  16.5 0.0 copy-done
  16.5 0.6 %copy-done.1 = f32[1,128]{1,0:T(1,128)S(1)} copy-done((f32[1,128]{1,0:T(1,128)S(1)}, f32[1,128]{1,0:T(1,128)}, u32[]{:S(2)}) %copy-start.1) | copy-done | bytes 536
  17.1 0.0 copy-done.2
  17.1 2.5 %queries.1 = (f32[256,1024]{1,0:T(8,128)S(1)}, bf16[256,1024]{1,0:T(8,128)(2,1)S(1)}, f32[1,128]{1,0:T(1,128)S(1)}, s32[1,8]{1,0:T(1,128)S(1)}) custom-call(bf16[256,1024]{1,0:T(8,128)(2,1)S(1)} %bitcast.10, bf16[256,1024]{1,0:T(8,128)(2,1)S(1)} %get-tuple-element.35.k_ref, f32[8,256]{1,0:T(8,128)S(1)} %get-tuple-element.36.beta_ref, ...), custom_call_target="tpu_custom_call" | custom-call | flops 2147483648 | bytes 4194304 | tf_op jit(solution)/shard_map/queries/pallas_call | solution.py:352
  19.6 0.0 collective-permute-done.2.refs_1_
  19.6 0.0 collective-permute-done.1.refs_0_
  19.6 0.4 enter.1
  20.0 0.1 collective-permute-start.3
  20.1 1.2 %rows_own.1 = (bf16[256,1024]{1,0:T(8,128)(2,1)S(1)}, bf16[16,8,1024]{2,1,0:T(8,128)(2,1)S(1)}) custom-call(s32[1]{0:T(128)} %bitcast.core_ref, bf16[512,128]{1,0:T(8,128)(2,1)S(1)} %get-tuple-element.54.state_ref, f32[256,1024]{1,0:T(8,128)S(1)} %get-tuple-element.50.local_ref, bf16[256,1024]{1,0:T(8,128)(2,1)S(1)} %get-tuple-element.51.reach_ref, ...), custom_call_target="tpu_custom_call" | custom-call | flops 2147483648 | bytes 4194304 | tf_op jit(solution)/shard_map/rows_own/pallas_call | solution.py:366
  21.2 0.2 collective-permute-done.3.state_ref
  21.4 1.1 %rows_other.1 = (bf16[256,1024]{1,0:T(8,128)(2,1)S(1)}, bf16[16,8,1024]{2,1,0:T(8,128)(2,1)S(1)}) custom-call(s32[1]{0:T(128)} %bitcast.core_ref, bf16[512,128]{1,0:T(8,128)(2,1)S(1)} %collective-permute-done.3.state_ref, f32[256,1024]{1,0:T(8,128)S(1)} %get-tuple-element.50.local_ref, ...), custom_call_target="tpu_custom_call", output_to_operand_aliasing={{0}: (7, {}), {1}: (8, {})} | custom-call | flops 67108864 | bytes 4194304 | tf_op jit(solution)/shard_map/rows_other/pallas_call | solution.py:369
  22.6 1.5 %collective-permute-start.4 = (bf16[256,1024]{1,0:T(8,128)(2,1)S(1)}, bf16[256,1024]{1,0:T(8,128)(2,1)S(1)}, u32[]{:S(2)}, u32[]{:S(2)}) collective-permute-start(bf16[256,1024]{1,0:T(8,128)(2,1)S(1)} %get-tuple-element.57), channel_id=1, source_target_pairs={{0,1},{1,0},{2,3},{3,2},{4,5},{5,4},{6,7},{7,6},{8,9},{9,8},{10,11... | collective-permute-start | bytes 1572872 | tf_op jit(solution)/shard_map/ppermute | solution.py:373
  24.1 18.8 %all_to_all.5.parts_ref = bf16[16,8,1024]{2,1,0:T(8,128)(2,1)S(1)} all-to-all(bf16[16,8,1024]{2,1,0:T(8,128)(2,1)S(1)} %get-tuple-element.58), channel_id=1, replica_groups=mesh['groups'=1,'ctx'=16,'pipe'=2,'dp'=1] {'ctx'}, dimensions={0} | all-to-all | bytes 524288 | tf_op jit(solution)/shard_map/all_to_all | solution.py:374
  42.9 0.8 %loss.1 = f32[1,8]{1,0:T(1,128)} custom-call(bf16[16,8,1024]{2,1,0:T(8,128)(2,1)S(1)} %all_to_all.5.parts_ref, s32[1,8]{1,0:T(1,128)S(1)} %get-tuple-element.59.pos_ref), custom_call_target="tpu_custom_call" | custom-call | bytes 4194304 | tf_op jit(solution)/shard_map/loss/pallas_call | solution.py:376
  43.7 0.0 collective-permute-done.4
  43.7 0.8 %copy.15 = bf16[1,1,256,1024]{3,2,1,0:T(8,128)(2,1)} copy(bf16[1,1,256,1024]{3,2,1,0:T(8,128)(2,1)S(1)} %bitcast.12) | data formatting | bytes 1048576
Async XLA Ops:
  6.2 10.3 %copy-start = (bf16[1,1,256,1024]{3,2,1,0:T(8,128)(2,1)S(1)}, bf16[1,1,256,1024]{3,2,1,0:T(8,128)(2,1)}, u32[]{:S(2)}) copy-start(bf16[1,1,256,1024]{3,2,1,0:T(8,128)(2,1)} %param.9) | copy-start | bytes 1572868
  6.2 1.7 %collective-permute-start = (bf16[1040,128]{1,0:T(8,128)(2,1)S(1)}, bf16[1040,128]{1,0:T(8,128)(2,1)S(1)}, u32[]{:S(2)}, u32[]{:S(2)}) collective-permute-start(bf16[1040,128]{1,0:T(8,128)(2,1)S(1)} %get-tuple-element.32), channel_id=1, source_target_pairs={{0,2},{2,0},{4,6},{6,4},{8,10},{10,8},{12,14},{14,12},{16,18},{18,... | collective-permute-start | bytes 798728 | tf_op jit(solution)/shard_map/ppermute | solution.py:331
  8.2 11.5 %collective-permute-start.1 = (bf16[1040,128]{1,0:T(8,128)(2,1)S(1)}, bf16[1040,128]{1,0:T(8,128)(2,1)S(1)}, u32[]{:S(2)}, u32[]{:S(2)}) collective-permute-start(bf16[1040,128]{1,0:T(8,128)(2,1)S(1)} %get-tuple-element.33), channel_id=1, source_target_pairs={{0,4},{2,6},{4,8},{6,10},{8,12},{10,14},{12,16},{14,18},{16,20},{1... | collective-permute-start | bytes 798728 | tf_op jit(solution)/shard_map/ppermute | solution.py:334
  13.0 6.6 %collective-permute-start.2 = (bf16[528,128]{1,0:T(8,128)(2,1)S(1)}, bf16[528,128]{1,0:T(8,128)(2,1)S(1)}, u32[]{:S(2)}, u32[]{:S(2)}) collective-permute-start(bf16[528,128]{1,0:T(8,128)(2,1)S(1)} %get-tuple-element.34), channel_id=1, source_target_pairs={{0,8},{2,10},{4,12},{6,14},{8,16},{10,18},{12,20},{14,22},{16,24},... | collective-permute-start | bytes 405512 | tf_op jit(solution)/shard_map/ppermute | solution.py:334
  16.5 0.7 %copy-start.1 = (f32[1,128]{1,0:T(1,128)S(1)}, f32[1,128]{1,0:T(1,128)}, u32[]{:S(2)}) copy-start(f32[1,128]{1,0:T(1,128)} %gain_in.1) | copy-start | bytes 1540
  16.5 0.7 %copy-start.2 = (s32[1,1,8]{2,1,0:T(1,128)S(1)}, s32[1,1,8]{2,1,0:T(1,128)}, u32[]{:S(2)}) copy-start(s32[1,1,8]{2,1,0:T(1,128)} %param.14) | copy-start | bytes 100
  20.0 1.4 %collective-permute-start.3 = (bf16[512,128]{1,0:T(8,128)(2,1)S(1)}, bf16[512,128]{1,0:T(8,128)(2,1)S(1)}, u32[]{:S(2)}, u32[]{:S(2)}) collective-permute-start(bf16[512,128]{1,0:T(8,128)(2,1)S(1)} %get-tuple-element.49), channel_id=1, source_target_pairs={{0,2},{2,0},{4,6},{6,4},{8,10},{10,8},{12,14},{14,12},{16,18},{18,... | collective-permute-start | bytes 393224 | tf_op jit(solution)/shard_map/ppermute | solution.py:331
  22.6 21.2 %collective-permute-start.4 = (bf16[256,1024]{1,0:T(8,128)(2,1)S(1)}, bf16[256,1024]{1,0:T(8,128)(2,1)S(1)}, u32[]{:S(2)}, u32[]{:S(2)}) collective-permute-start(bf16[256,1024]{1,0:T(8,128)(2,1)S(1)} %get-tuple-element.57), channel_id=1, source_target_pairs={{0,1},{1,0},{2,3},{3,2},{4,5},{5,4},{6,7},{7,6},{8,9},{9,8},{10,11... | collective-permute-start | bytes 1572872 | tf_op jit(solution)/shard_map/ppermute | solution.py:373

commit v4 on v3

--- a/solution.py
+++ b/solution.py
@@ -263,7 +263,7 @@
 
 
 def rows_kernel(
-    heads, ndoc, copies, own, core_ref, state_ref, local_ref, reach_ref, v_ref, gain_ref, ids_ref, *refs
+    heads, ndoc, own, core_ref, state_ref, local_ref, reach_ref, v_ref, gain_ref, ids_ref, *refs
 ):
     out_ref, pooled_ref = refs[-2:]
     half = heads // 2
@@ -271,19 +271,17 @@
     docs = lax.broadcasted_iota(jnp.int32, (ndoc, v_ref.shape[0]), 0)
     onehot = (docs == ids_ref[...]).astype(F32).astype(BF16)
     gain = gain_ref[...]
+    mean = jnp.full((SUB, SUB), 1.0 / SUB, BF16)
     for h in range(half):
         cols = pl.ds(pl.multiple_of((group * half + h) * SUB, SUB), SUB)
         o = local_ref[:, cols] + dot(reach_ref[:, cols], state_ref[h * SUB : (h + 1) * SUB, :])
-        scale = lax.rsqrt(jnp.sum(o * o, axis=-1, keepdims=True) * (1.0 / SUB) + 1e-06)
+        scale = lax.rsqrt(dot1(o * o, mean) + 1e-06)
         out = (v_ref[:, cols].astype(F32) + o * scale * gain).astype(BF16)
         out_ref[:, cols] = out
-        pooled = dot(onehot, out).astype(BF16)
-        for i in range(copies):
-            pooled_ref[i, :, cols] = pooled
-
-
-def score(emb, cands, own, pos):
-    scores = dot(cands, emb, NT, HIGHEST) / 0.05
+        pooled_ref[:, cols] = dot(onehot, out).astype(BF16)
+
+
+def losses(scores, own, pos):
     cidx = lax.broadcasted_iota(jnp.int32, scores.shape, 0)
     didx = lax.broadcasted_iota(jnp.int32, scores.shape, 1)
     total = jnp.sum(jnp.where(cidx != own + didx, jnp.exp(scores), 0.0), axis=0, keepdims=True)
@@ -291,9 +289,35 @@
     return jnp.log(total) - picked
 
 
-def loss_kernel(parts_ref, pos_ref, loss_ref):
-    emb = unit(jnp.sum(parts_ref[...].astype(F32), axis=0))
-    loss_ref[...] = score(emb, emb, 0, pos_ref[...])
+def add_kernel(a_ref, b_ref, out_ref):
+    total = (a_ref[...].astype(F32) + b_ref[...].astype(F32)).astype(BF16)
+    for i in range(out_ref.shape[0]):
+        out_ref[i] = total
+
+
+def store_rows(rows_ref, out_ref, sems):
+    pieces = sems.shape[0]
+    step = rows_ref.shape[0] // pieces
+    at = [pl.ds(i * step, step) for i in range(pieces)]
+    return [pltpu.make_async_copy(rows_ref.at[x, :], out_ref.at[x, :], sems.at[i]) for i, x in enumerate(at)]
+
+
+def final_kernel(parts_ref, pos_ref, rows_ref, loss_out, out_ref, loss_ref, sems, loss_sem):
+    copies = store_rows(rows_ref, out_ref, sems)
+    for copy in copies:
+        copy.start()
+    sums = jnp.sum(parts_ref[...].astype(F32), axis=0)
+    gram = dot(sums, sums, NT, HIGHEST)
+    cidx = lax.broadcasted_iota(jnp.int32, gram.shape, 0)
+    didx = lax.broadcasted_iota(jnp.int32, gram.shape, 1)
+    squares = jnp.where(cidx == didx, gram, 0.0)
+    across = lax.rsqrt(jnp.sum(squares, axis=0, keepdims=True) + 1e-06)
+    down = lax.rsqrt(jnp.sum(squares, axis=1, keepdims=True) + 1e-06)
+    loss_ref[...] = losses(gram * across * down / 0.05, 0, pos_ref[...])
+    copies.append(pltpu.make_async_copy(loss_ref, loss_out, loss_sem))
+    copies[-1].start()
+    for copy in copies:
+        copy.wait()
 
 
 VMEM = pl.BlockSpec(memory_space=pltpu.VMEM)
@@ -361,23 +385,35 @@
         "enter", [SMEM] + [VMEM] * (2 + reach), 1 << 25,
     )(core, keep, got, *arrived)
     theirs = swapped(give)
-    outs = [((length, width), BF16), ((size, ndoc, width), BF16)]
+    outs = [((length, width), BF16), ((ndoc, width), BF16)]
     rest = (local, reached, v, gain, ids)
     begun = call(
-        functools.partial(rows_kernel, heads, ndoc, size, True), outs, "rows_own", [SMEM] + [VMEM] * 6, 1 << 31
+        functools.partial(rows_kernel, heads, ndoc, True), outs, "rows_own", [SMEM] + [VMEM] * 6, 1 << 31
     )(core, mine, *rest)
     rows_out, pooled = call(
-        functools.partial(rows_kernel, heads, ndoc, size, False), outs, "rows_other",
+        functools.partial(rows_kernel, heads, ndoc, False), outs, "rows_other",
         [SMEM] + [VMEM] * 8, 1 << 26, aliases={7: 0, 8: 1},
     )(core, theirs, *rest, *begun)
     passed = lax.ppermute(rows_out, "pipe", [(i, (i + 1) % pipes) for i in range(pipes)])
-    parts = lax.all_to_all(pooled, "ctx", 0, 0)
+    (sums,) = call(add_kernel, [((chips, ndoc, width), BF16)], "sums", [VMEM, VMEM])(pooled, swapped(pooled))
+    sides = [list(range(i, size, 2)) for i in range(2)]
+    parts = lax.all_to_all(sums, "ctx", 0, 0, axis_index_groups=sides)
     if replicas == 1:
-        (loss,) = call(loss_kernel, [((1, ndoc), F32)], "loss", [VMEM, VMEM])(parts, pos)
+        loss, passed = pl.pallas_call(
+            final_kernel,
+            out_shape=[pltpu.HBM((1, ndoc), F32), pltpu.HBM(passed.shape, passed.dtype)],
+            in_specs=[VMEM] * 3,
+            out_specs=[HBM, HBM],
+            scratch_shapes=[
+                pltpu.VMEM((1, ndoc), F32), pltpu.SemaphoreType.DMA((8,)), pltpu.SemaphoreType.DMA
+            ],
+            compiler_params=pltpu.CompilerParams(vmem_limit_bytes=40 << 20),
+            name="final",
+        )(parts, pos, passed)
     else:
         mine = unit(jnp.sum(parts.astype(F32), axis=0))
         cands = lax.all_gather(mine.astype(BF16), "dp", axis=0, tiled=True).astype(F32)
-        loss = score(mine, cands, lax.axis_index("dp") * ndoc, pos)
+        loss = losses(dot(cands, mine, NT, HIGHEST) / 0.05, lax.axis_index("dp") * ndoc, pos)
     return (passed.reshape(1, 1, length, width), loss.reshape(1, 1, ndoc))
 
 

time: 44.8 us -> 42.3 us (0.944)
  blocking collectives: 18.8 us -> 16 us
  waiting for transfers between devices: 1.36 us -> 2.74 us
  local copies, waits for them, and re-layouts: 1.45 us -> 0.65 us
    all_to_all x1, blocking collectives: 18.8 us -> 16 us  [on_device(): parts = lax.all_to_all(sums, 'ctx', 0, 0, axis_index_groups=sides)]
    ppermute x2 -> x3, waiting for transfers between devices: 1.35 us -> 2.74 us  [swapped(): return lax.ppermute(x, 'ctx', [(i, i ^ 1) for i in range(size)])]
    unnamed x7 -> x6, local copies, waits for them, and re-layouts: 1.45 us -> 0.65 us
    pallas_call x3 -> x4, Pallas kernels: 3.14 us -> 2.8 us  [the longest x1 0.95 us: on_device(): call(functools.partial(rows_kernel, heads, ndoc, True), outs, 'rows_own',...]
  transfers between devices with their start and end apart: 5 -> 6, of which waited for: 2 -> 3; matrix products, arithmetic and copies ran while one was open for 0% -> 0% of each run, Pallas kernels for 10% -> 8%
where the time goes in v4:
time: 42.3 us; the launch traced here: 42 us
  blocking collectives  16 us (38%)
  Pallas kernels  11.5 us (27%)
  starting transfers between devices  10.4 us (25%)
  waiting for transfers between devices  2.74 us (6%)
  between operations  0.75 us (2%)
  local copies, waits for them, and re-layouts  0.65 us (2%)
    all_to_all x1, blocking collectives, on_device(): parts = lax.all_to_all(sums, 'ctx', 0, 0, axis_index_groups=sides)  16 us
    ppermute x2, starting transfers between devices, from_behind(): return lax.ppermute(x, 'ctx', [(i, i + 2 * d) for i in range(size - 2 * d)])  8.28 us
    pallas_call x1, Pallas kernels, on_device(): call(functools.partial(chunk_kernel, heads, subs), [(big, BF16), (big, BF...  5.59 us
    ppermute x3, waiting for transfers between devices, swapped(): return lax.ppermute(x, 'ctx', [(i, i ^ 1) for i in range(size)])  2.74 us
    pallas_call x1, Pallas kernels, on_device(): call(functools.partial(query_kernel, heads, subs), [((length, width), F32...  2.48 us
    ppermute x1, starting transfers between devices, on_device(): lax.ppermute(rows_out, 'pipe', [(i, (i + 1) % pipes) for i in range(pipes)])  1.5 us
    pallas_call x1, Pallas kernels, on_device(): call(functools.partial(rows_kernel, heads, ndoc, True), outs, 'rows_own',...  0.95 us
    pallas_call x1, Pallas kernels, on_device(): call(functools.partial(rows_kernel, heads, ndoc, False), outs, 'rows_othe...  0.95 us
  transfers between devices with their start and end apart: 6, of which 3 were waited for; matrix products, arithmetic and copies ran while one was open for 0% of the time, Pallas kernels for 8%

profile of v4, /device:TPU:0, one launch (start us, length us, event | category | flops | bytes accessed | tf_op | source)
XLA Modules:
  0.0 42.0 jit_solution(722673283179949083)
XLA Ops:
  0.6 5.6 %chunks.1 = (bf16[1040,128]{1,0:T(8,128)(2,1)S(1)}, bf16[1040,128]{1,0:T(8,128)(2,1)S(1)}, f32[256,1024]{1,0:T(8,128)S(1)}, bf16[256,1024]{1,0:T(8,128)(2,1)S(1)...) custom-call(s32[1]{0:T(128)} %bitcast.core_ref, ...), custom_call_target="tpu_custom_call" | custom-call | flops 2147483648 | bytes 4194304 | tf_op jit(solution)/shard_map/chunks/pallas_call | solution.py:361
  6.2 0.0 copy-start
  6.3 0.5 %collective-permute-start = (bf16[1040,128]{1,0:T(8,128)(2,1)S(1)}, bf16[1040,128]{1,0:T(8,128)(2,1)S(1)}, u32[]{:S(2)}, u32[]{:S(2)}) collective-permute-start(bf16[1040,128]{1,0:T(8,128)(2,1)S(1)} %get-tuple-element.34), channel_id=1, source_target_pairs={{0,2},{2,0},{4,6},{6,4},{8,10},{10,8},{12,14},{14,12},{16,18},{18,... | collective-permute-start | bytes 798728 | tf_op jit(solution)/shard_map/ppermute | solution.py:355
  6.8 1.2 %collective-permute-done.got_ref = bf16[1040,128]{1,0:T(8,128)(2,1)S(1)} collective-permute-done((bf16[1040,128]{1,0:T(8,128)(2,1)S(1)}, bf16[1040,128]{1,0:T(8,128)(2,1)S(1)}, u32[]{:S(2)}, u32[]{:S(2)}) %collective-permute-start) | collective-permute-done | bytes 266272 | tf_op jit(solution)/shard_map/ppermute | solution.py:355
  7.9 0.2 pair.1
  8.2 4.8 %collective-permute-start.1 = (bf16[1040,128]{1,0:T(8,128)(2,1)S(1)}, bf16[1040,128]{1,0:T(8,128)(2,1)S(1)}, u32[]{:S(2)}, u32[]{:S(2)}) collective-permute-start(bf16[1040,128]{1,0:T(8,128)(2,1)S(1)} %get-tuple-element.35), channel_id=1, source_target_pairs={{0,4},{2,6},{4,8},{6,10},{8,12},{10,14},{12,16},{14,18},{16,20},{1... | collective-permute-start | bytes 798728 | tf_op jit(solution)/shard_map/ppermute | solution.py:358
  13.0 3.5 %collective-permute-start.2 = (bf16[528,128]{1,0:T(8,128)(2,1)S(1)}, bf16[528,128]{1,0:T(8,128)(2,1)S(1)}, u32[]{:S(2)}, u32[]{:S(2)}) collective-permute-start(bf16[528,128]{1,0:T(8,128)(2,1)S(1)} %get-tuple-element.36), channel_id=1, source_target_pairs={{0,8},{2,10},{4,12},{6,14},{8,16},{10,18},{12,20},{14,22},{16,24},... | collective-permute-start | bytes 405512 | tf_op jit(solution)/shard_map/ppermute | solution.py:358
  16.5 0.0 copy-start.1
  16.5 0.0 copy-start.2
  16.5 0.0 copy-done
  16.5 0.6 %copy-done.1 = f32[1,128]{1,0:T(1,128)S(1)} copy-done((f32[1,128]{1,0:T(1,128)S(1)}, f32[1,128]{1,0:T(1,128)}, u32[]{:S(2)}) %copy-start.1) | copy-done | bytes 536
  17.1 0.0 copy-done.2
  17.1 2.5 %queries.1 = (f32[256,1024]{1,0:T(8,128)S(1)}, bf16[256,1024]{1,0:T(8,128)(2,1)S(1)}, f32[1,128]{1,0:T(1,128)S(1)}, s32[1,8]{1,0:T(1,128)S(1)}) custom-call(bf16[256,1024]{1,0:T(8,128)(2,1)S(1)} %bitcast.10, bf16[256,1024]{1,0:T(8,128)(2,1)S(1)} %get-tuple-element.37.k_ref, f32[8,256]{1,0:T(8,128)S(1)} %get-tuple-element.38.beta_ref, ...), custom_call_target="tpu_custom_call" | custom-call | flops 2147483648 | bytes 4194304 | tf_op jit(solution)/shard_map/queries/pallas_call | solution.py:376
  19.6 0.0 collective-permute-done.2.refs_1_
  19.6 0.0 collective-permute-done.1.refs_0_
  19.7 0.4 enter.1
  20.0 0.1 collective-permute-start.3
  20.1 0.9 %rows_own.1 = (bf16[256,1024]{1,0:T(8,128)(2,1)S(1)}, bf16[8,1024]{1,0:T(8,128)(2,1)S(1)}) custom-call(s32[1]{0:T(128)} %bitcast.core_ref, bf16[512,128]{1,0:T(8,128)(2,1)S(1)} %get-tuple-element.56.state_ref, f32[256,1024]{1,0:T(8,128)S(1)} %get-tuple-element.52.local_ref, bf16[256,1024]{1,0:T(8,128)(2,1)S(1)} %get-tuple-element.53.reach_ref, ...), custom_call_target="tpu_custom_call" | custom-call | flops 2147483648 | bytes 4194304 | tf_op jit(solution)/shard_map/rows_own/pallas_call | solution.py:390
  21.0 0.4 collective-permute-done.3.state_ref
  21.4 0.9 %rows_other.1 = (bf16[256,1024]{1,0:T(8,128)(2,1)S(1)}, bf16[8,1024]{1,0:T(8,128)(2,1)S(1)}) custom-call(s32[1]{0:T(128)} %bitcast.core_ref, bf16[512,128]{1,0:T(8,128)(2,1)S(1)} %collective-permute-done.3.state_ref, f32[256,1024]{1,0:T(8,128)S(1)} %get-tuple-element.52.local_ref, ...), custom_call_target="tpu_custom_call", output_to_operand_aliasing={{0}: (7, {}), {1}: (8, {})} | custom-call | flops 67108864 | bytes 4194304 | tf_op jit(solution)/shard_map/rows_other/pallas_call | solution.py:393
  22.4 1.5 %collective-permute-start.5 = (bf16[256,1024]{1,0:T(8,128)(2,1)S(1)}, bf16[256,1024]{1,0:T(8,128)(2,1)S(1)}, u32[]{:S(2)}, u32[]{:S(2)}) collective-permute-start(bf16[256,1024]{1,0:T(8,128)(2,1)S(1)} %get-tuple-element.61), channel_id=1, source_target_pairs={{0,1},{1,0},{2,3},{3,2},{4,5},{5,4},{6,7},{7,6},{8,9},{9,8},{10,11... | collective-permute-start | bytes 1572872 | tf_op jit(solution)/shard_map/ppermute | solution.py:397
  23.9 0.0 collective-permute-start.4
  23.9 1.2 %collective-permute-done.4.b_ref = bf16[8,1024]{1,0:T(8,128)(2,1)S(1)} collective-permute-done((bf16[8,1024]{1,0:T(8,128)(2,1)S(1)}, bf16[8,1024]{1,0:T(8,128)(2,1)S(1)}, u32[]{:S(2)}, u32[]{:S(2)}) %collective-permute-start.4) | collective-permute-done | bytes 16416 | tf_op jit(solution)/shard_map/ppermute | solution.py:355
  25.1 16.0 %all_to_all.5.parts_ref = bf16[8,8,1024]{2,1,0:T(8,128)(2,1)S(1)} all-to-all(bf16[8,8,1024]{2,1,0:T(8,128)(2,1)S(1)} %sums.1), channel_id=1, replica_groups={{0,4,8,12,16,20,24,28},{2,6,10,14,18,22,26,30},{1,5,9,13,17,21,25,29},{..., dimensions={0} | all-to-all | bytes 262144 | tf_op jit(solution)/shard_map/all_to_all | solution.py:400
  41.1 0.0 collective-permute-done.5.rows_ref
  41.1 0.9 %final.1 = (f32[1,8]{1,0:T(1,128)}, bf16[256,1024]{1,0:T(8,128)(2,1)}) custom-call(bf16[8,8,1024]{2,1,0:T(8,128)(2,1)S(1)} %all_to_all.5.parts_ref, s32[1,8]{1,0:T(1,128)S(1)} %get-tuple-element.60.pos_ref, bf16[256,1024]{1,0:T(8,128)(2,1)S(1)} %collective-permute-done.5.rows_ref), custom_call_target="tpu_custom_call" | custom-call | tf_op jit(solution)/shard_map/final/pallas_call | solution.py:402
  (1 shorter events, 0.0 us)
Async XLA Ops:
  6.2 10.3 %copy-start = (bf16[1,1,256,1024]{3,2,1,0:T(8,128)(2,1)S(1)}, bf16[1,1,256,1024]{3,2,1,0:T(8,128)(2,1)}, u32[]{:S(2)}) copy-start(bf16[1,1,256,1024]{3,2,1,0:T(8,128)(2,1)} %param.9) | copy-start | bytes 1572868
  6.3 1.7 %collective-permute-start = (bf16[1040,128]{1,0:T(8,128)(2,1)S(1)}, bf16[1040,128]{1,0:T(8,128)(2,1)S(1)}, u32[]{:S(2)}, u32[]{:S(2)}) collective-permute-start(bf16[1040,128]{1,0:T(8,128)(2,1)S(1)} %get-tuple-element.34), channel_id=1, source_target_pairs={{0,2},{2,0},{4,6},{6,4},{8,10},{10,8},{12,14},{14,12},{16,18},{18,... | collective-permute-start | bytes 798728 | tf_op jit(solution)/shard_map/ppermute | solution.py:355
  8.2 11.5 %collective-permute-start.1 = (bf16[1040,128]{1,0:T(8,128)(2,1)S(1)}, bf16[1040,128]{1,0:T(8,128)(2,1)S(1)}, u32[]{:S(2)}, u32[]{:S(2)}) collective-permute-start(bf16[1040,128]{1,0:T(8,128)(2,1)S(1)} %get-tuple-element.35), channel_id=1, source_target_pairs={{0,4},{2,6},{4,8},{6,10},{8,12},{10,14},{12,16},{14,18},{16,20},{1... | collective-permute-start | bytes 798728 | tf_op jit(solution)/shard_map/ppermute | solution.py:358
  13.0 6.6 %collective-permute-start.2 = (bf16[528,128]{1,0:T(8,128)(2,1)S(1)}, bf16[528,128]{1,0:T(8,128)(2,1)S(1)}, u32[]{:S(2)}, u32[]{:S(2)}) collective-permute-start(bf16[528,128]{1,0:T(8,128)(2,1)S(1)} %get-tuple-element.36), channel_id=1, source_target_pairs={{0,8},{2,10},{4,12},{6,14},{8,16},{10,18},{12,20},{14,22},{16,24},... | collective-permute-start | bytes 405512 | tf_op jit(solution)/shard_map/ppermute | solution.py:358
  16.5 0.7 %copy-start.1 = (f32[1,128]{1,0:T(1,128)S(1)}, f32[1,128]{1,0:T(1,128)}, u32[]{:S(2)}) copy-start(f32[1,128]{1,0:T(1,128)} %gain_in.1) | copy-start | bytes 1540
  16.5 0.7 %copy-start.2 = (s32[1,1,8]{2,1,0:T(1,128)S(1)}, s32[1,1,8]{2,1,0:T(1,128)}, u32[]{:S(2)}) copy-start(s32[1,1,8]{2,1,0:T(1,128)} %param.14) | copy-start | bytes 100
  20.0 1.4 %collective-permute-start.3 = (bf16[512,128]{1,0:T(8,128)(2,1)S(1)}, bf16[512,128]{1,0:T(8,128)(2,1)S(1)}, u32[]{:S(2)}, u32[]{:S(2)}) collective-permute-start(bf16[512,128]{1,0:T(8,128)(2,1)S(1)} %get-tuple-element.51), channel_id=1, source_target_pairs={{0,2},{2,0},{4,6},{6,4},{8,10},{10,8},{12,14},{14,12},{16,18},{18,... | collective-permute-start | bytes 393224 | tf_op jit(solution)/shard_map/ppermute | solution.py:355
  22.4 18.7 %collective-permute-start.5 = (bf16[256,1024]{1,0:T(8,128)(2,1)S(1)}, bf16[256,1024]{1,0:T(8,128)(2,1)S(1)}, u32[]{:S(2)}, u32[]{:S(2)}) collective-permute-start(bf16[256,1024]{1,0:T(8,128)(2,1)S(1)} %get-tuple-element.61), channel_id=1, source_target_pairs={{0,1},{1,0},{2,3},{3,2},{4,5},{5,4},{6,7},{7,6},{8,9},{9,8},{10,11... | collective-permute-start | bytes 1572872 | tf_op jit(solution)/shard_map/ppermute | solution.py:397
  23.9 1.2 %collective-permute-start.4 = (bf16[8,1024]{1,0:T(8,128)(2,1)S(1)}, bf16[8,1024]{1,0:T(8,128)(2,1)S(1)}, u32[]{:S(2)}, u32[]{:S(2)}) collective-permute-start(bf16[8,1024]{1,0:T(8,128)(2,1)S(1)} %get-tuple-element.59.a_ref), channel_id=1, source_target_pairs={{0,2},{2,0},{4,6},{6,4},{8,10},{10,8},{12,14},{14,12},{16,18},{18,... | collective-permute-start | bytes 49160 | tf_op jit(solution)/shard_map/ppermute | solution.py:355

commit v5 on v4

--- a/solution.py
+++ b/solution.py
@@ -249,15 +249,19 @@
         marks.append(ends(ref, (heads if d < reach - 1 else half) * SUB))
     links = [(marks[d][0] == marks[d + 1][1]).astype(F32) for d in range(reach)]
     joined = (early[1] == late[0]).astype(F32)
-    for h in range(half):
-        at, up = slice(h * SUB, (h + 1) * SUB), slice((half + h) * SUB, (half + h + 1) * SUB)
-        state = chips[-1][at, :].astype(F32)
-        for d in range(reach - 2, -1, -1):
-            state = chips[d][up, :].astype(F32) + links[d + 1] * dot1(chips[d][at, :], state)
-        state = (links[0] * state).astype(BF16)
-        p1 = jnp.where(first, keep_ref[at, :], got_ref[at, :])
+    ats = [slice(h * SUB, (h + 1) * SUB) for h in range(half)]
+    ups = [slice((half + h) * SUB, (half + h + 1) * SUB) for h in range(half)]
+    states = [chips[-1][at, :].astype(F32) for at in ats]
+    for d in range(reach - 2, -1, -1):
+        moved = [dot1(chips[d][at, :], state) for at, state in zip(ats, states)]
+        states = [chips[d][up, :].astype(F32) + links[d + 1] * x for up, x in zip(ups, moved)]
+    states = [(links[0] * state).astype(BF16) for state in states]
+    moved = [
+        dot(jnp.where(first, keep_ref[at, :], got_ref[at, :]), state) for at, state in zip(ats, states)
+    ]
+    for at, up, state, x in zip(ats, ups, states, moved):
         u1 = jnp.where(first, keep_ref[up, :], got_ref[up, :])
-        middle = (joined * (u1.astype(F32) + dot(p1, state))).astype(BF16)
+        middle = (joined * (u1.astype(F32) + x)).astype(BF16)
         send_ref[at, :] = jnp.where(first, middle, state)
         mine_ref[at, :] = jnp.where(first, state, middle)
 
@@ -272,13 +276,19 @@
     onehot = (docs == ids_ref[...]).astype(F32).astype(BF16)
     gain = gain_ref[...]
     mean = jnp.full((SUB, SUB), 1.0 / SUB, BF16)
-    for h in range(half):
-        cols = pl.ds(pl.multiple_of((group * half + h) * SUB, SUB), SUB)
-        o = local_ref[:, cols] + dot(reach_ref[:, cols], state_ref[h * SUB : (h + 1) * SUB, :])
-        scale = lax.rsqrt(dot1(o * o, mean) + 1e-06)
-        out = (v_ref[:, cols].astype(F32) + o * scale * gain).astype(BF16)
-        out_ref[:, cols] = out
-        pooled_ref[:, cols] = dot(onehot, out).astype(BF16)
+    cols = [pl.ds(pl.multiple_of((group * half + h) * SUB, SUB), SUB) for h in range(half)]
+    outs = [
+        local_ref[:, x] + dot(reach_ref[:, x], state_ref[h * SUB : (h + 1) * SUB, :])
+        for h, x in enumerate(cols)
+    ]
+    scales = [lax.rsqrt(dot1(o * o, mean) + 1e-06) * gain for o in outs]
+    outs = [
+        (v_ref[:, x].astype(F32) + o * scale).astype(BF16) for x, o, scale in zip(cols, outs, scales)
+    ]
+    sums = [dot(onehot, out).astype(BF16) for out in outs]
+    for x, out, pooled in zip(cols, outs, sums):
+        out_ref[:, x] = out
+        pooled_ref[:, x] = pooled
 
 
 def losses(scores, own, pos):

time: 42.3 us -> 41.9 us (level)
  Pallas kernels: 11.5 us -> 10.7 us
  transfers between devices with their start and end apart: 6 -> 6, of which waited for: 3 -> 3; matrix products, arithmetic and copies ran while one was open for 0% -> 0% of each run, Pallas kernels for 8% -> 7%
where the time goes in v5:
time: 41.9 us; the launch traced here: 41.6 us
  blocking collectives  16 us (38%)
  Pallas kernels  10.7 us (26%)
  starting transfers between devices  10.4 us (25%)
  waiting for transfers between devices  3.13 us (7%)
  between operations  0.75 us (2%)
  local copies, waits for them, and re-layouts  0.65 us (2%)
    all_to_all x1, blocking collectives, on_device(): parts = lax.all_to_all(sums, 'ctx', 0, 0, axis_index_groups=sides)  16 us
    ppermute x2, starting transfers between devices, from_behind(): return lax.ppermute(x, 'ctx', [(i, i + 2 * d) for i in range(size - 2 * d)])  8.28 us
    pallas_call x1, Pallas kernels, on_device(): call(functools.partial(chunk_kernel, heads, subs), [(big, BF16), (big, BF...  5.59 us
    ppermute x3, waiting for transfers between devices, swapped(): return lax.ppermute(x, 'ctx', [(i, i ^ 1) for i in range(size)])  3.12 us
    pallas_call x1, Pallas kernels, on_device(): call(functools.partial(query_kernel, heads, subs), [((length, width), F32...  2.48 us
    ppermute x1, starting transfers between devices, on_device(): lax.ppermute(rows_out, 'pipe', [(i, (i + 1) % pipes) for i in range(pipes)])  1.5 us
    pallas_call x1, Pallas kernels, on_device(): pl.pallas_call(final_kernel, out_shape=[pltpu.HBM((1, ndoc), F32), pltpu....  0.89 us
  transfers between devices with their start and end apart: 6, of which 3 were waited for; matrix products, arithmetic and copies ran while one was open for 0% of the time, Pallas kernels for 7%

profile of v5, /device:TPU:0, one launch (start us, length us, event | category | flops | bytes accessed | tf_op | source)
XLA Modules:
  0.0 41.6 jit_solution(3158276919183330813)
XLA Ops:
  0.6 5.6 %chunks.1 = (bf16[1040,128]{1,0:T(8,128)(2,1)S(1)}, bf16[1040,128]{1,0:T(8,128)(2,1)S(1)}, f32[256,1024]{1,0:T(8,128)S(1)}, bf16[256,1024]{1,0:T(8,128)(2,1)S(1)...) custom-call(s32[1]{0:T(128)} %bitcast.core_ref, ...), custom_call_target="tpu_custom_call" | custom-call | flops 2147483648 | bytes 4194304 | tf_op jit(solution)/shard_map/chunks/pallas_call | solution.py:371
  6.2 0.0 copy-start
  6.3 0.5 %collective-permute-start = (bf16[1040,128]{1,0:T(8,128)(2,1)S(1)}, bf16[1040,128]{1,0:T(8,128)(2,1)S(1)}, u32[]{:S(2)}, u32[]{:S(2)}) collective-permute-start(bf16[1040,128]{1,0:T(8,128)(2,1)S(1)} %get-tuple-element.34), channel_id=1, source_target_pairs={{0,2},{2,0},{4,6},{6,4},{8,10},{10,8},{12,14},{14,12},{16,18},{18,... | collective-permute-start | bytes 798728 | tf_op jit(solution)/shard_map/ppermute | solution.py:365
  6.8 1.2 %collective-permute-done.got_ref = bf16[1040,128]{1,0:T(8,128)(2,1)S(1)} collective-permute-done((bf16[1040,128]{1,0:T(8,128)(2,1)S(1)}, bf16[1040,128]{1,0:T(8,128)(2,1)S(1)}, u32[]{:S(2)}, u32[]{:S(2)}) %collective-permute-start) | collective-permute-done | bytes 266272 | tf_op jit(solution)/shard_map/ppermute | solution.py:365
  7.9 0.2 pair.1
  8.2 4.8 %collective-permute-start.1 = (bf16[1040,128]{1,0:T(8,128)(2,1)S(1)}, bf16[1040,128]{1,0:T(8,128)(2,1)S(1)}, u32[]{:S(2)}, u32[]{:S(2)}) collective-permute-start(bf16[1040,128]{1,0:T(8,128)(2,1)S(1)} %get-tuple-element.35), channel_id=1, source_target_pairs={{0,4},{2,6},{4,8},{6,10},{8,12},{10,14},{12,16},{14,18},{16,20},{1... | collective-permute-start | bytes 798728 | tf_op jit(solution)/shard_map/ppermute | solution.py:368
  13.0 3.5 %collective-permute-start.2 = (bf16[528,128]{1,0:T(8,128)(2,1)S(1)}, bf16[528,128]{1,0:T(8,128)(2,1)S(1)}, u32[]{:S(2)}, u32[]{:S(2)}) collective-permute-start(bf16[528,128]{1,0:T(8,128)(2,1)S(1)} %get-tuple-element.36), channel_id=1, source_target_pairs={{0,8},{2,10},{4,12},{6,14},{8,16},{10,18},{12,20},{14,22},{16,24},... | collective-permute-start | bytes 405512 | tf_op jit(solution)/shard_map/ppermute | solution.py:368
  16.5 0.0 copy-start.1
  16.5 0.0 copy-start.2
  16.5 0.0 copy-done
  16.5 0.6 %copy-done.1 = f32[1,128]{1,0:T(1,128)S(1)} copy-done((f32[1,128]{1,0:T(1,128)S(1)}, f32[1,128]{1,0:T(1,128)}, u32[]{:S(2)}) %copy-start.1) | copy-done | bytes 536
  17.1 0.0 copy-done.2
  17.1 2.5 %queries.1 = (f32[256,1024]{1,0:T(8,128)S(1)}, bf16[256,1024]{1,0:T(8,128)(2,1)S(1)}, f32[1,128]{1,0:T(1,128)S(1)}, s32[1,8]{1,0:T(1,128)S(1)}) custom-call(bf16[256,1024]{1,0:T(8,128)(2,1)S(1)} %bitcast.10, bf16[256,1024]{1,0:T(8,128)(2,1)S(1)} %get-tuple-element.37.k_ref, f32[8,256]{1,0:T(8,128)S(1)} %get-tuple-element.38.beta_ref, ...), custom_call_target="tpu_custom_call" | custom-call | flops 2147483648 | bytes 4194304 | tf_op jit(solution)/shard_map/queries/pallas_call | solution.py:386
  19.6 0.0 collective-permute-done.2.refs_1_
  19.6 0.0 collective-permute-done.1.refs_0_
  19.7 0.4 enter.1
  20.0 0.1 collective-permute-start.3
  20.1 0.6 %rows_own.1 = (bf16[256,1024]{1,0:T(8,128)(2,1)S(1)}, bf16[8,1024]{1,0:T(8,128)(2,1)S(1)}) custom-call(s32[1]{0:T(128)} %bitcast.core_ref, bf16[512,128]{1,0:T(8,128)(2,1)S(1)} %get-tuple-element.56.state_ref, f32[256,1024]{1,0:T(8,128)S(1)} %get-tuple-element.52.local_ref, bf16[256,1024]{1,0:T(8,128)(2,1)S(1)} %get-tuple-element.53.reach_ref, ...), custom_call_target="tpu_custom_call" | custom-call | flops 2147483648 | bytes 4194304 | tf_op jit(solution)/shard_map/rows_own/pallas_call | solution.py:400
  20.7 0.8 %collective-permute-done.3.state_ref = bf16[512,128]{1,0:T(8,128)(2,1)S(1)} collective-permute-done((bf16[512,128]{1,0:T(8,128)(2,1)S(1)}, bf16[512,128]{1,0:T(8,128)(2,1)S(1)}, u32[]{:S(2)}, u32[]{:S(2)}) %collective-permute-start.3) | collective-permute-done | bytes 131104 | tf_op jit(solution)/shard_map/ppermute | solution.py:365
  21.4 0.6 %rows_other.1 = (bf16[256,1024]{1,0:T(8,128)(2,1)S(1)}, bf16[8,1024]{1,0:T(8,128)(2,1)S(1)}) custom-call(s32[1]{0:T(128)} %bitcast.core_ref, bf16[512,128]{1,0:T(8,128)(2,1)S(1)} %collective-permute-done.3.state_ref, f32[256,1024]{1,0:T(8,128)S(1)} %get-tuple-element.52.local_ref, ...), custom_call_target="tpu_custom_call", output_to_operand_aliasing={{0}: (7, {}), {1}: (8, {})} | custom-call | flops 67108864 | bytes 4194304 | tf_op jit(solution)/shard_map/rows_other/pallas_call | solution.py:403
  22.0 1.5 %collective-permute-start.5 = (bf16[256,1024]{1,0:T(8,128)(2,1)S(1)}, bf16[256,1024]{1,0:T(8,128)(2,1)S(1)}, u32[]{:S(2)}, u32[]{:S(2)}) collective-permute-start(bf16[256,1024]{1,0:T(8,128)(2,1)S(1)} %get-tuple-element.61), channel_id=1, source_target_pairs={{0,1},{1,0},{2,3},{3,2},{4,5},{5,4},{6,7},{7,6},{8,9},{9,8},{10,11... | collective-permute-start | bytes 1572872 | tf_op jit(solution)/shard_map/ppermute | solution.py:407
  23.5 0.0 collective-permute-start.4
  23.5 1.2 %collective-permute-done.4.b_ref = bf16[8,1024]{1,0:T(8,128)(2,1)S(1)} collective-permute-done((bf16[8,1024]{1,0:T(8,128)(2,1)S(1)}, bf16[8,1024]{1,0:T(8,128)(2,1)S(1)}, u32[]{:S(2)}, u32[]{:S(2)}) %collective-permute-start.4) | collective-permute-done | bytes 16416 | tf_op jit(solution)/shard_map/ppermute | solution.py:365
  24.7 16.0 %all_to_all.5.parts_ref = bf16[8,8,1024]{2,1,0:T(8,128)(2,1)S(1)} all-to-all(bf16[8,8,1024]{2,1,0:T(8,128)(2,1)S(1)} %sums.1), channel_id=1, replica_groups={{0,4,8,12,16,20,24,28},{2,6,10,14,18,22,26,30},{1,5,9,13,17,21,25,29},{..., dimensions={0} | all-to-all | bytes 262144 | tf_op jit(solution)/shard_map/all_to_all | solution.py:410
  40.7 0.0 collective-permute-done.5.rows_ref
  40.7 0.9 %final.1 = (f32[1,8]{1,0:T(1,128)}, bf16[256,1024]{1,0:T(8,128)(2,1)}) custom-call(bf16[8,8,1024]{2,1,0:T(8,128)(2,1)S(1)} %all_to_all.5.parts_ref, s32[1,8]{1,0:T(1,128)S(1)} %get-tuple-element.60.pos_ref, bf16[256,1024]{1,0:T(8,128)(2,1)S(1)} %collective-permute-done.5.rows_ref), custom_call_target="tpu_custom_call" | custom-call | tf_op jit(solution)/shard_map/final/pallas_call | solution.py:412
  (1 shorter events, 0.0 us)
Async XLA Ops:
  6.2 10.3 %copy-start = (bf16[1,1,256,1024]{3,2,1,0:T(8,128)(2,1)S(1)}, bf16[1,1,256,1024]{3,2,1,0:T(8,128)(2,1)}, u32[]{:S(2)}) copy-start(bf16[1,1,256,1024]{3,2,1,0:T(8,128)(2,1)} %param.9) | copy-start | bytes 1572868
  6.3 1.7 %collective-permute-start = (bf16[1040,128]{1,0:T(8,128)(2,1)S(1)}, bf16[1040,128]{1,0:T(8,128)(2,1)S(1)}, u32[]{:S(2)}, u32[]{:S(2)}) collective-permute-start(bf16[1040,128]{1,0:T(8,128)(2,1)S(1)} %get-tuple-element.34), channel_id=1, source_target_pairs={{0,2},{2,0},{4,6},{6,4},{8,10},{10,8},{12,14},{14,12},{16,18},{18,... | collective-permute-start | bytes 798728 | tf_op jit(solution)/shard_map/ppermute | solution.py:365
  8.2 11.5 %collective-permute-start.1 = (bf16[1040,128]{1,0:T(8,128)(2,1)S(1)}, bf16[1040,128]{1,0:T(8,128)(2,1)S(1)}, u32[]{:S(2)}, u32[]{:S(2)}) collective-permute-start(bf16[1040,128]{1,0:T(8,128)(2,1)S(1)} %get-tuple-element.35), channel_id=1, source_target_pairs={{0,4},{2,6},{4,8},{6,10},{8,12},{10,14},{12,16},{14,18},{16,20},{1... | collective-permute-start | bytes 798728 | tf_op jit(solution)/shard_map/ppermute | solution.py:368
  13.0 6.6 %collective-permute-start.2 = (bf16[528,128]{1,0:T(8,128)(2,1)S(1)}, bf16[528,128]{1,0:T(8,128)(2,1)S(1)}, u32[]{:S(2)}, u32[]{:S(2)}) collective-permute-start(bf16[528,128]{1,0:T(8,128)(2,1)S(1)} %get-tuple-element.36), channel_id=1, source_target_pairs={{0,8},{2,10},{4,12},{6,14},{8,16},{10,18},{12,20},{14,22},{16,24},... | collective-permute-start | bytes 405512 | tf_op jit(solution)/shard_map/ppermute | solution.py:368
  16.5 0.7 %copy-start.1 = (f32[1,128]{1,0:T(1,128)S(1)}, f32[1,128]{1,0:T(1,128)}, u32[]{:S(2)}) copy-start(f32[1,128]{1,0:T(1,128)} %gain_in.1) | copy-start | bytes 1540
  16.5 0.7 %copy-start.2 = (s32[1,1,8]{2,1,0:T(1,128)S(1)}, s32[1,1,8]{2,1,0:T(1,128)}, u32[]{:S(2)}) copy-start(s32[1,1,8]{2,1,0:T(1,128)} %param.14) | copy-start | bytes 100
  20.0 1.4 %collective-permute-start.3 = (bf16[512,128]{1,0:T(8,128)(2,1)S(1)}, bf16[512,128]{1,0:T(8,128)(2,1)S(1)}, u32[]{:S(2)}, u32[]{:S(2)}) collective-permute-start(bf16[512,128]{1,0:T(8,128)(2,1)S(1)} %get-tuple-element.51), channel_id=1, source_target_pairs={{0,2},{2,0},{4,6},{6,4},{8,10},{10,8},{12,14},{14,12},{16,18},{18,... | collective-permute-start | bytes 393224 | tf_op jit(solution)/shard_map/ppermute | solution.py:365
  22.0 18.7 %collective-permute-start.5 = (bf16[256,1024]{1,0:T(8,128)(2,1)S(1)}, bf16[256,1024]{1,0:T(8,128)(2,1)S(1)}, u32[]{:S(2)}, u32[]{:S(2)}) collective-permute-start(bf16[256,1024]{1,0:T(8,128)(2,1)S(1)} %get-tuple-element.61), channel_id=1, source_target_pairs={{0,1},{1,0},{2,3},{3,2},{4,5},{5,4},{6,7},{7,6},{8,9},{9,8},{10,11... | collective-permute-start | bytes 1572872 | tf_op jit(solution)/shard_map/ppermute | solution.py:407
  23.5 1.2 %collective-permute-start.4 = (bf16[8,1024]{1,0:T(8,128)(2,1)S(1)}, bf16[8,1024]{1,0:T(8,128)(2,1)S(1)}, u32[]{:S(2)}, u32[]{:S(2)}) collective-permute-start(bf16[8,1024]{1,0:T(8,128)(2,1)S(1)} %get-tuple-element.59.a_ref), channel_id=1, source_target_pairs={{0,2},{2,0},{4,6},{6,4},{8,10},{10,8},{12,14},{14,12},{16,18},{18,... | collective-permute-start | bytes 49160 | tf_op jit(solution)/shard_map/ppermute | solution.py:365

commit v6 on v5

--- a/solution.py
+++ b/solution.py
@@ -34,6 +34,11 @@
 def dot3(a, b, dims=NN):
     (ah, al), (bh, bl) = split(a), split(b)
     return dot(ah, bh, dims) + (dot(al, bh, dims) + dot(ah, bl, dims))
+
+
+def dot2(a, b):
+    high, low = split(b)
+    return dot(a, high) + dot(a, low)
 
 
 def unit(x):
@@ -153,14 +158,13 @@
         pp[h, j] = decay.lead[i : i + 1, SUB - 1 :] * eye - got[:, SUB:]
         uu[h, j] = got[:, :SUB] + (dot(dl, wh) + dot(dh, wl))
     for h in range(heads):
-        p0, u0 = pp[h, 0].astype(BF16), uu[h, 0].astype(BF16)
-        p0_ref[h * SUB : (h + 1) * SUB, :] = p0
-        u0_ref[h * SUB : (h + 1) * SUB, :] = u0
-        for j in range(1, subs):
-            got = dot1(pp[h, j], jnp.concatenate([u0, p0], axis=1))
+        p0_ref[h * SUB : (h + 1) * SUB, :] = pp[h, 0]
+        u0_ref[h * SUB : (h + 1) * SUB, :] = uu[h, 0]
+    for j in range(1, subs):
+        for h in range(heads):
+            got = dot2(pp[h, j].astype(BF16), jnp.concatenate([uu[h, 0], pp[h, 0]], axis=1))
             uu[h, 0] = uu[h, j] + got[:, :SUB]
             pp[h, 0] = got[:, SUB:]
-            u0, p0 = uu[h, 0].astype(BF16), pp[h, 0].astype(BF16)
     half_heads = heads // 2
     first = core_ref[0] == 0
     for h in range(half_heads):
@@ -201,12 +205,14 @@
         local[h, j] = dot(ah, wh) + (dot(al, wh) + dot(ah, wl))
     for h, j in chains:
         if j > 0:
-            rb = reach[h, j].astype(BF16)
             at = slice(h * SUB, (h + 1) * SUB)
-            local[h, j] = local[h, j] + dot(rb, u0_ref[at, :])
-            reach[h, j] = dot(rb, p0_ref[at, :])
-        local_ref[j * SUB : (j + 1) * SUB, h * SUB : (h + 1) * SUB] = local[h, j]
-        reach_ref[j * SUB : (j + 1) * SUB, h * SUB : (h + 1) * SUB] = reach[h, j].astype(BF16)
+            got = dot3(reach[h, j], jnp.concatenate([u0_ref[at, :], p0_ref[at, :]], axis=1))
+            local[h, j] = local[h, j] + got[:, :SUB]
+            reach[h, j] = got[:, SUB:]
+    for h, j in chains:
+        rows, cols = slice(j * SUB, (j + 1) * SUB), slice(h * SUB, (h + 1) * SUB)
+        local_ref[rows, cols] = local[h, j]
+        reach_ref[0, rows, cols], reach_ref[1, rows, cols] = split(reach[h, j])
 
 
 def ends(ref, rows):
@@ -253,15 +259,15 @@
     ups = [slice((half + h) * SUB, (half + h + 1) * SUB) for h in range(half)]
     states = [chips[-1][at, :].astype(F32) for at in ats]
     for d in range(reach - 2, -1, -1):
-        moved = [dot1(chips[d][at, :], state) for at, state in zip(ats, states)]
+        moved = [dot2(chips[d][at, :], state) for at, state in zip(ats, states)]
         states = [chips[d][up, :].astype(F32) + links[d + 1] * x for up, x in zip(ups, moved)]
-    states = [(links[0] * state).astype(BF16) for state in states]
+    states = [links[0] * state for state in states]
     moved = [
-        dot(jnp.where(first, keep_ref[at, :], got_ref[at, :]), state) for at, state in zip(ats, states)
+        dot2(jnp.where(first, keep_ref[at, :], got_ref[at, :]), state) for at, state in zip(ats, states)
     ]
     for at, up, state, x in zip(ats, ups, states, moved):
         u1 = jnp.where(first, keep_ref[up, :], got_ref[up, :])
-        middle = (joined * (u1.astype(F32) + x)).astype(BF16)
+        middle = joined * (u1.astype(F32) + x)
         send_ref[at, :] = jnp.where(first, middle, state)
         mine_ref[at, :] = jnp.where(first, state, middle)
 
@@ -277,10 +283,11 @@
     gain = gain_ref[...]
     mean = jnp.full((SUB, SUB), 1.0 / SUB, BF16)
     cols = [pl.ds(pl.multiple_of((group * half + h) * SUB, SUB), SUB) for h in range(half)]
-    outs = [
-        local_ref[:, x] + dot(reach_ref[:, x], state_ref[h * SUB : (h + 1) * SUB, :])
-        for h, x in enumerate(cols)
-    ]
+    outs = []
+    for h, x in enumerate(cols):
+        high, low = split(state_ref[h * SUB : (h + 1) * SUB, :])
+        near, rest = reach_ref[0, :, x], reach_ref[1, :, x]
+        outs.append(local_ref[:, x] + (dot(near, high) + (dot(rest, high) + dot(near, low))))
     scales = [lax.rsqrt(dot1(o * o, mean) + 1e-06) * gain for o in outs]
     outs = [
         (v_ref[:, x].astype(F32) + o * scale).astype(BF16) for x, o, scale in zip(cols, outs, scales)
@@ -371,7 +378,7 @@
     send, keep, wv, yy, p0, u0, k, v, beta, gate, ids = call(
         functools.partial(chunk_kernel, heads, subs),
         [(big, BF16), (big, BF16), ((length, width), F32), ((length, width), BF16)]
-        + [((heads * SUB, SUB), BF16)] * 2 + [((length, width), BF16)] * 2
+        + [((heads * SUB, SUB), F32)] * 2 + [((length, width), BF16)] * 2
         + [((heads, length), F32)] * 2 + [((1, length), jnp.int32)],
         "chunks", [SMEM] + [HBM] * 5, 1 << 31,
         [pltpu.SemaphoreType.DMA((3 + 2 * subs,))],
@@ -385,13 +392,13 @@
     arrived = [from_behind(full, d) for d in range(1, reach)] + [from_behind(tail, reach)]
     local, reached, gain, pos = call(
         functools.partial(query_kernel, heads, subs),
-        [((length, width), F32), ((length, width), BF16), (norm_gain.shape, F32), ((1, ndoc), jnp.int32)],
+        [((length, width), F32), ((2, length, width), BF16), (norm_gain.shape, F32), ((1, ndoc), jnp.int32)],
         "queries", [VMEM] * 11, 1 << 31,
     )(q, k, beta, gate, ids, wv, yy, p0, u0, norm_gain, positives[0])
     arrived, local, reached, gain, pos = lax.optimization_barrier((arrived, local, reached, gain, pos))
     give, mine = call(
         functools.partial(enter_kernel, heads, reach),
-        [((half * SUB, SUB), BF16)] * 2,
+        [((half * SUB, SUB), F32)] * 2,
         "enter", [SMEM] + [VMEM] * (2 + reach), 1 << 25,
     )(core, keep, got, *arrived)
     theirs = swapped(give)

time: 41.9 us -> 42.4 us (1.012)
  Pallas kernels: 10.7 us -> 11.4 us
  transfers between devices with their start and end apart: 6 -> 6, of which waited for: 3 -> 3; matrix products, arithmetic and copies ran while one was open for 0% -> 0% of each run, Pallas kernels for 7% -> 8%
where the time goes in v6:
time: 42.4 us; the launch traced here: 42.1 us
  blocking collectives  15.8 us (37%)
  Pallas kernels  11.4 us (27%)
  starting transfers between devices  10.4 us (25%)
  waiting for transfers between devices  3.2 us (8%)
  between operations  0.75 us (2%)
  local copies, waits for them, and re-layouts  0.65 us (2%)
    all_to_all x1, blocking collectives, on_device(): parts = lax.all_to_all(sums, 'ctx', 0, 0, axis_index_groups=sides)  15.8 us
    ppermute x2, starting transfers between devices, from_behind(): return lax.ppermute(x, 'ctx', [(i, i + 2 * d) for i in range(size - 2 * d)])  8.28 us
    pallas_call x1, Pallas kernels, on_device(): call(functools.partial(chunk_kernel, heads, subs), [(big, BF16), (big, BF...  5.71 us
    ppermute x3, waiting for transfers between devices, swapped(): return lax.ppermute(x, 'ctx', [(i, i ^ 1) for i in range(size)])  3.19 us
    pallas_call x1, Pallas kernels, on_device(): call(functools.partial(query_kernel, heads, subs), [((length, width), F32...  2.74 us
    ppermute x1, starting transfers between devices, on_device(): lax.ppermute(rows_out, 'pipe', [(i, (i + 1) % pipes) for i in range(pipes)])  1.5 us
    pallas_call x1, Pallas kernels, on_device(): pl.pallas_call(final_kernel, out_shape=[pltpu.HBM((1, ndoc), F32), pltpu....  0.89 us
  transfers between devices with their start and end apart: 6, of which 3 were waited for; matrix products, arithmetic and copies ran while one was open for 0% of the time, Pallas kernels for 8%

profile of v6, /device:TPU:0, one launch (start us, length us, event | category | flops | bytes accessed | tf_op | source)
XLA Modules:
  0.0 42.1 jit_solution(12144620451372209654)
XLA Ops:
  0.6 5.7 %chunks.1 = (bf16[1040,128]{1,0:T(8,128)(2,1)S(1)}, bf16[1040,128]{1,0:T(8,128)(2,1)S(1)}, f32[256,1024]{1,0:T(8,128)S(1)}, bf16[256,1024]{1,0:T(8,128)(2,1)S(1)...) custom-call(s32[1]{0:T(128)} %bitcast.core_ref, ...), custom_call_target="tpu_custom_call" | custom-call | flops 2147483648 | bytes 4194304 | tf_op jit(solution)/shard_map/chunks/pallas_call | solution.py:378
  6.4 0.0 copy-start
  6.4 0.5 %collective-permute-start = (bf16[1040,128]{1,0:T(8,128)(2,1)S(1)}, bf16[1040,128]{1,0:T(8,128)(2,1)S(1)}, u32[]{:S(2)}, u32[]{:S(2)}) collective-permute-start(bf16[1040,128]{1,0:T(8,128)(2,1)S(1)} %get-tuple-element.34), channel_id=1, source_target_pairs={{0,2},{2,0},{4,6},{6,4},{8,10},{10,8},{12,14},{14,12},{16,18},{18,... | collective-permute-start | bytes 798728 | tf_op jit(solution)/shard_map/ppermute | solution.py:372
  6.9 1.2 %collective-permute-done.got_ref = bf16[1040,128]{1,0:T(8,128)(2,1)S(1)} collective-permute-done((bf16[1040,128]{1,0:T(8,128)(2,1)S(1)}, bf16[1040,128]{1,0:T(8,128)(2,1)S(1)}, u32[]{:S(2)}, u32[]{:S(2)}) %collective-permute-start) | collective-permute-done | bytes 266272 | tf_op jit(solution)/shard_map/ppermute | solution.py:372
  8.1 0.2 pair.1
  8.3 4.8 %collective-permute-start.1 = (bf16[1040,128]{1,0:T(8,128)(2,1)S(1)}, bf16[1040,128]{1,0:T(8,128)(2,1)S(1)}, u32[]{:S(2)}, u32[]{:S(2)}) collective-permute-start(bf16[1040,128]{1,0:T(8,128)(2,1)S(1)} %get-tuple-element.35), channel_id=1, source_target_pairs={{0,4},{2,6},{4,8},{6,10},{8,12},{10,14},{12,16},{14,18},{16,20},{1... | collective-permute-start | bytes 798728 | tf_op jit(solution)/shard_map/ppermute | solution.py:375
  13.1 3.5 %collective-permute-start.2 = (bf16[528,128]{1,0:T(8,128)(2,1)S(1)}, bf16[528,128]{1,0:T(8,128)(2,1)S(1)}, u32[]{:S(2)}, u32[]{:S(2)}) collective-permute-start(bf16[528,128]{1,0:T(8,128)(2,1)S(1)} %get-tuple-element.36), channel_id=1, source_target_pairs={{0,8},{2,10},{4,12},{6,14},{8,16},{10,18},{12,20},{14,22},{16,24},... | collective-permute-start | bytes 405512 | tf_op jit(solution)/shard_map/ppermute | solution.py:375
  16.6 0.0 copy-start.1
  16.6 0.0 copy-start.2
  16.6 0.0 copy-done
  16.6 0.6 %copy-done.1 = f32[1,128]{1,0:T(1,128)S(1)} copy-done((f32[1,128]{1,0:T(1,128)S(1)}, f32[1,128]{1,0:T(1,128)}, u32[]{:S(2)}) %copy-start.1) | copy-done | bytes 536
  17.3 0.0 copy-done.2
  17.3 2.7 %queries.1 = (f32[256,1024]{1,0:T(8,128)S(1)}, bf16[2,256,1024]{2,1,0:T(8,128)(2,1)S(1)}, f32[1,128]{1,0:T(1,128)S(1)}, s32[1,8]{1,0:T(1,128)S(1)}) custom-call(bf16[256,1024]{1,0:T(8,128)(2,1)S(1)} %bitcast.10, bf16[256,1024]{1,0:T(8,128)(2,1)S(1)} %get-tuple-element.37.k_ref, f32[8,256]{1,0:T(8,128)S(1)} %get-tuple-element.38.beta_ref, ...), custom_call_target="tpu_custom_call" | custom-call | flops 2147483648 | bytes 4194304 | tf_op jit(solution)/shard_map/queries/pallas_call | solution.py:393
  20.0 0.0 collective-permute-done.2.refs_1_
  20.0 0.0 collective-permute-done.1.refs_0_
  20.0 0.4 %enter.1 = (f32[512,128]{1,0:T(8,128)S(1)}, f32[512,128]{1,0:T(8,128)S(1)}) custom-call(s32[1]{0:T(128)} %bitcast.core_ref, bf16[1040,128]{1,0:T(8,128)(2,1)S(1)} %get-tuple-element.33.keep_ref, bf16[1040,128]{1,0:T(8,128)(2,1)S(1)} %collective-permute-done.got_ref, bf16[1040,128]{1,0:T(8,128)(2,1)S(1)} %collective-permute-done.1.refs_0_, ...), custom_call_target="tpu_custom_call" | custom-call | flops 33554432 | bytes 4194304 | tf_op jit(solution)/shard_map/enter/pallas_call | solution.py:399
  20.5 0.1 collective-permute-start.3
  20.5 0.7 %rows_own.1 = (bf16[256,1024]{1,0:T(8,128)(2,1)S(1)}, bf16[8,1024]{1,0:T(8,128)(2,1)S(1)}) custom-call(s32[1]{0:T(128)} %bitcast.core_ref, f32[512,128]{1,0:T(8,128)S(1)} %get-tuple-element.56.state_ref, f32[256,1024]{1,0:T(8,128)S(1)} %get-tuple-element.52.local_ref, bf16[2,256,1024]{2,1,0:T(8,128)(2,1)S(1)} %get-tuple-element.53.reach_ref, ...), custom_call_target="tpu_custom_call" | custom-call | flops 2147483648 | bytes 4194304 | tf_op jit(solution)/shard_map/rows_own/pallas_call | solution.py:407
  21.2 0.8 %collective-permute-done.3.state_ref = f32[512,128]{1,0:T(8,128)S(1)} collective-permute-done((f32[512,128]{1,0:T(8,128)S(1)}, f32[512,128]{1,0:T(8,128)S(1)}, u32[]{:S(2)}, u32[]{:S(2)}) %collective-permute-start.3) | collective-permute-done | bytes 262176 | tf_op jit(solution)/shard_map/ppermute | solution.py:372
  22.1 0.7 %rows_other.1 = (bf16[256,1024]{1,0:T(8,128)(2,1)S(1)}, bf16[8,1024]{1,0:T(8,128)(2,1)S(1)}) custom-call(s32[1]{0:T(128)} %bitcast.core_ref, f32[512,128]{1,0:T(8,128)S(1)} %collective-permute-done.3.state_ref, f32[256,1024]{1,0:T(8,128)S(1)} %get-tuple-element.52.local_ref, ...), custom_call_target="tpu_custom_call", output_to_operand_aliasing={{0}: (7, {}), {1}: (8, {})} | custom-call | flops 67108864 | bytes 4194304 | tf_op jit(solution)/shard_map/rows_other/pallas_call | solution.py:410
  22.7 1.5 %collective-permute-start.5 = (bf16[256,1024]{1,0:T(8,128)(2,1)S(1)}, bf16[256,1024]{1,0:T(8,128)(2,1)S(1)}, u32[]{:S(2)}, u32[]{:S(2)}) collective-permute-start(bf16[256,1024]{1,0:T(8,128)(2,1)S(1)} %get-tuple-element.61), channel_id=1, source_target_pairs={{0,1},{1,0},{2,3},{3,2},{4,5},{5,4},{6,7},{7,6},{8,9},{9,8},{10,11... | collective-permute-start | bytes 1572872 | tf_op jit(solution)/shard_map/ppermute | solution.py:414
  24.2 0.0 collective-permute-start.4
  24.2 1.2 %collective-permute-done.4.b_ref = bf16[8,1024]{1,0:T(8,128)(2,1)S(1)} collective-permute-done((bf16[8,1024]{1,0:T(8,128)(2,1)S(1)}, bf16[8,1024]{1,0:T(8,128)(2,1)S(1)}, u32[]{:S(2)}, u32[]{:S(2)}) %collective-permute-start.4) | collective-permute-done | bytes 16416 | tf_op jit(solution)/shard_map/ppermute | solution.py:372
  25.4 15.8 %all_to_all.5.parts_ref = bf16[8,8,1024]{2,1,0:T(8,128)(2,1)S(1)} all-to-all(bf16[8,8,1024]{2,1,0:T(8,128)(2,1)S(1)} %sums.1), channel_id=1, replica_groups={{0,4,8,12,16,20,24,28},{2,6,10,14,18,22,26,30},{1,5,9,13,17,21,25,29},{..., dimensions={0} | all-to-all | bytes 262144 | tf_op jit(solution)/shard_map/all_to_all | solution.py:417
  41.2 0.0 collective-permute-done.5.rows_ref
  41.2 0.9 %final.1 = (f32[1,8]{1,0:T(1,128)}, bf16[256,1024]{1,0:T(8,128)(2,1)}) custom-call(bf16[8,8,1024]{2,1,0:T(8,128)(2,1)S(1)} %all_to_all.5.parts_ref, s32[1,8]{1,0:T(1,128)S(1)} %get-tuple-element.60.pos_ref, bf16[256,1024]{1,0:T(8,128)(2,1)S(1)} %collective-permute-done.5.rows_ref), custom_call_target="tpu_custom_call" | custom-call | tf_op jit(solution)/shard_map/final/pallas_call | solution.py:419
  (1 shorter events, 0.0 us)
Async XLA Ops:
  6.4 10.3 %copy-start = (bf16[1,1,256,1024]{3,2,1,0:T(8,128)(2,1)S(1)}, bf16[1,1,256,1024]{3,2,1,0:T(8,128)(2,1)}, u32[]{:S(2)}) copy-start(bf16[1,1,256,1024]{3,2,1,0:T(8,128)(2,1)} %param.9) | copy-start | bytes 1572868
  6.4 1.7 %collective-permute-start = (bf16[1040,128]{1,0:T(8,128)(2,1)S(1)}, bf16[1040,128]{1,0:T(8,128)(2,1)S(1)}, u32[]{:S(2)}, u32[]{:S(2)}) collective-permute-start(bf16[1040,128]{1,0:T(8,128)(2,1)S(1)} %get-tuple-element.34), channel_id=1, source_target_pairs={{0,2},{2,0},{4,6},{6,4},{8,10},{10,8},{12,14},{14,12},{16,18},{18,... | collective-permute-start | bytes 798728 | tf_op jit(solution)/shard_map/ppermute | solution.py:372
  8.3 11.7 %collective-permute-start.1 = (bf16[1040,128]{1,0:T(8,128)(2,1)S(1)}, bf16[1040,128]{1,0:T(8,128)(2,1)S(1)}, u32[]{:S(2)}, u32[]{:S(2)}) collective-permute-start(bf16[1040,128]{1,0:T(8,128)(2,1)S(1)} %get-tuple-element.35), channel_id=1, source_target_pairs={{0,4},{2,6},{4,8},{6,10},{8,12},{10,14},{12,16},{14,18},{16,20},{1... | collective-permute-start | bytes 798728 | tf_op jit(solution)/shard_map/ppermute | solution.py:375
  13.1 6.9 %collective-permute-start.2 = (bf16[528,128]{1,0:T(8,128)(2,1)S(1)}, bf16[528,128]{1,0:T(8,128)(2,1)S(1)}, u32[]{:S(2)}, u32[]{:S(2)}) collective-permute-start(bf16[528,128]{1,0:T(8,128)(2,1)S(1)} %get-tuple-element.36), channel_id=1, source_target_pairs={{0,8},{2,10},{4,12},{6,14},{8,16},{10,18},{12,20},{14,22},{16,24},... | collective-permute-start | bytes 405512 | tf_op jit(solution)/shard_map/ppermute | solution.py:375
  16.6 0.7 %copy-start.1 = (f32[1,128]{1,0:T(1,128)S(1)}, f32[1,128]{1,0:T(1,128)}, u32[]{:S(2)}) copy-start(f32[1,128]{1,0:T(1,128)} %gain_in.1) | copy-start | bytes 1540
  16.6 0.7 %copy-start.2 = (s32[1,1,8]{2,1,0:T(1,128)S(1)}, s32[1,1,8]{2,1,0:T(1,128)}, u32[]{:S(2)}) copy-start(s32[1,1,8]{2,1,0:T(1,128)} %param.14) | copy-start | bytes 100
  20.5 1.6 %collective-permute-start.3 = (f32[512,128]{1,0:T(8,128)S(1)}, f32[512,128]{1,0:T(8,128)S(1)}, u32[]{:S(2)}, u32[]{:S(2)}) collective-permute-start(f32[512,128]{1,0:T(8,128)S(1)} %get-tuple-element.51), channel_id=1, source_target_pairs={{0,2},{2,0},{4,6},{6,4},{8,10},{10,8},{12,14},{14,12},{16,18},{18,... | collective-permute-start | bytes 786440 | tf_op jit(solution)/shard_map/ppermute | solution.py:372
  22.7 18.5 %collective-permute-start.5 = (bf16[256,1024]{1,0:T(8,128)(2,1)S(1)}, bf16[256,1024]{1,0:T(8,128)(2,1)S(1)}, u32[]{:S(2)}, u32[]{:S(2)}) collective-permute-start(bf16[256,1024]{1,0:T(8,128)(2,1)S(1)} %get-tuple-element.61), channel_id=1, source_target_pairs={{0,1},{1,0},{2,3},{3,2},{4,5},{5,4},{6,7},{7,6},{8,9},{9,8},{10,11... | collective-permute-start | bytes 1572872 | tf_op jit(solution)/shard_map/ppermute | solution.py:414
  24.2 1.2 %collective-permute-start.4 = (bf16[8,1024]{1,0:T(8,128)(2,1)S(1)}, bf16[8,1024]{1,0:T(8,128)(2,1)S(1)}, u32[]{:S(2)}, u32[]{:S(2)}) collective-permute-start(bf16[8,1024]{1,0:T(8,128)(2,1)S(1)} %get-tuple-element.59.a_ref), channel_id=1, source_target_pairs={{0,2},{2,0},{4,6},{6,4},{8,10},{10,8},{12,14},{14,12},{16,18},{18,... | collective-permute-start | bytes 49160 | tf_op jit(solution)/shard_map/ppermute | solution.py:372

commit v7 on v6

--- a/solution.py
+++ b/solution.py
@@ -212,7 +212,7 @@
     for h, j in chains:
         rows, cols = slice(j * SUB, (j + 1) * SUB), slice(h * SUB, (h + 1) * SUB)
         local_ref[rows, cols] = local[h, j]
-        reach_ref[0, rows, cols], reach_ref[1, rows, cols] = split(reach[h, j])
+        reach_ref[rows, 2 * h * SUB : 2 * (h + 1) * SUB] = jnp.concatenate(split(reach[h, j]), axis=1)
 
 
 def ends(ref, rows):
@@ -286,8 +286,10 @@
     outs = []
     for h, x in enumerate(cols):
         high, low = split(state_ref[h * SUB : (h + 1) * SUB, :])
-        near, rest = reach_ref[0, :, x], reach_ref[1, :, x]
-        outs.append(local_ref[:, x] + (dot(near, high) + (dot(rest, high) + dot(near, low))))
+        wide = pl.ds(pl.multiple_of((group * half + h) * 2 * SUB, 2 * SUB), 2 * SUB)
+        near = reach_ref[:, wide]
+        moved = dot(near, jnp.concatenate([high, high], axis=0)) + dot(near[:, :SUB], low)
+        outs.append(local_ref[:, x] + moved)
     scales = [lax.rsqrt(dot1(o * o, mean) + 1e-06) * gain for o in outs]
     outs = [
         (v_ref[:, x].astype(F32) + o * scale).astype(BF16) for x, o, scale in zip(cols, outs, scales)
@@ -392,7 +394,7 @@
     arrived = [from_behind(full, d) for d in range(1, reach)] + [from_behind(tail, reach)]
     local, reached, gain, pos = call(
         functools.partial(query_kernel, heads, subs),
-        [((length, width), F32), ((2, length, width), BF16), (norm_gain.shape, F32), ((1, ndoc), jnp.int32)],
+        [((length, width), F32), ((length, 2 * width), BF16), (norm_gain.shape, F32), ((1, ndoc), jnp.int32)],
         "queries", [VMEM] * 11, 1 << 31,
     )(q, k, beta, gate, ids, wv, yy, p0, u0, norm_gain, positives[0])
     arrived, local, reached, gain, pos = lax.optimization_barrier((arrived, local, reached, gain, pos))

time: 42.4 us -> 42.4 us (level)
  no operation moved by 1% of the time
where the time goes in v7:
time: 42.4 us; the launch traced here: 42.1 us
  blocking collectives  15.8 us (37%)
  Pallas kernels  11.3 us (27%)
  starting transfers between devices  10.4 us (25%)
  waiting for transfers between devices  3.23 us (8%)
  between operations  0.75 us (2%)
  local copies, waits for them, and re-layouts  0.65 us (2%)
    all_to_all x1, blocking collectives, on_device(): parts = lax.all_to_all(sums, 'ctx', 0, 0, axis_index_groups=sides)  15.8 us
    ppermute x2, starting transfers between devices, from_behind(): return lax.ppermute(x, 'ctx', [(i, i + 2 * d) for i in range(size - 2 * d)])  8.28 us
    pallas_call x1, Pallas kernels, on_device(): call(functools.partial(chunk_kernel, heads, subs), [(big, BF16), (big, BF...  5.71 us
    ppermute x3, waiting for transfers between devices, swapped(): return lax.ppermute(x, 'ctx', [(i, i ^ 1) for i in range(size)])  3.22 us
    pallas_call x1, Pallas kernels, on_device(): call(functools.partial(query_kernel, heads, subs), [((length, width), F32...  2.73 us
    ppermute x1, starting transfers between devices, on_device(): lax.ppermute(rows_out, 'pipe', [(i, (i + 1) % pipes) for i in range(pipes)])  1.5 us
    pallas_call x1, Pallas kernels, on_device(): pl.pallas_call(final_kernel, out_shape=[pltpu.HBM((1, ndoc), F32), pltpu....  0.89 us
  transfers between devices with their start and end apart: 6, of which 3 were waited for; matrix products, arithmetic and copies ran while one was open for 0% of the time, Pallas kernels for 8%

profile of v7, /device:TPU:0, one launch (start us, length us, event | category | flops | bytes accessed | tf_op | source)
XLA Modules:
  0.0 42.1 jit_solution(15770964394282750379)
XLA Ops:
  0.6 5.7 %chunks.1 = (bf16[1040,128]{1,0:T(8,128)(2,1)S(1)}, bf16[1040,128]{1,0:T(8,128)(2,1)S(1)}, f32[256,1024]{1,0:T(8,128)S(1)}, bf16[256,1024]{1,0:T(8,128)(2,1)S(1)...) custom-call(s32[1]{0:T(128)} %bitcast.core_ref, ...), custom_call_target="tpu_custom_call" | custom-call | flops 2147483648 | bytes 4194304 | tf_op jit(solution)/shard_map/chunks/pallas_call | solution.py:380
  6.4 0.0 copy-start
  6.4 0.5 %collective-permute-start = (bf16[1040,128]{1,0:T(8,128)(2,1)S(1)}, bf16[1040,128]{1,0:T(8,128)(2,1)S(1)}, u32[]{:S(2)}, u32[]{:S(2)}) collective-permute-start(bf16[1040,128]{1,0:T(8,128)(2,1)S(1)} %get-tuple-element.34), channel_id=1, source_target_pairs={{0,2},{2,0},{4,6},{6,4},{8,10},{10,8},{12,14},{14,12},{16,18},{18,... | collective-permute-start | bytes 798728 | tf_op jit(solution)/shard_map/ppermute | solution.py:374
  6.9 1.2 %collective-permute-done.got_ref = bf16[1040,128]{1,0:T(8,128)(2,1)S(1)} collective-permute-done((bf16[1040,128]{1,0:T(8,128)(2,1)S(1)}, bf16[1040,128]{1,0:T(8,128)(2,1)S(1)}, u32[]{:S(2)}, u32[]{:S(2)}) %collective-permute-start) | collective-permute-done | bytes 266272 | tf_op jit(solution)/shard_map/ppermute | solution.py:374
  8.1 0.2 pair.1
  8.3 4.8 %collective-permute-start.1 = (bf16[1040,128]{1,0:T(8,128)(2,1)S(1)}, bf16[1040,128]{1,0:T(8,128)(2,1)S(1)}, u32[]{:S(2)}, u32[]{:S(2)}) collective-permute-start(bf16[1040,128]{1,0:T(8,128)(2,1)S(1)} %get-tuple-element.35), channel_id=1, source_target_pairs={{0,4},{2,6},{4,8},{6,10},{8,12},{10,14},{12,16},{14,18},{16,20},{1... | collective-permute-start | bytes 798728 | tf_op jit(solution)/shard_map/ppermute | solution.py:377
  13.1 3.5 %collective-permute-start.2 = (bf16[528,128]{1,0:T(8,128)(2,1)S(1)}, bf16[528,128]{1,0:T(8,128)(2,1)S(1)}, u32[]{:S(2)}, u32[]{:S(2)}) collective-permute-start(bf16[528,128]{1,0:T(8,128)(2,1)S(1)} %get-tuple-element.36), channel_id=1, source_target_pairs={{0,8},{2,10},{4,12},{6,14},{8,16},{10,18},{12,20},{14,22},{16,24},... | collective-permute-start | bytes 405512 | tf_op jit(solution)/shard_map/ppermute | solution.py:377
  16.6 0.0 copy-start.1
  16.6 0.0 copy-start.2
  16.6 0.0 copy-done
  16.6 0.6 %copy-done.1 = f32[1,128]{1,0:T(1,128)S(1)} copy-done((f32[1,128]{1,0:T(1,128)S(1)}, f32[1,128]{1,0:T(1,128)}, u32[]{:S(2)}) %copy-start.1) | copy-done | bytes 536
  17.3 0.0 copy-done.2
  17.3 2.7 %queries.1 = (f32[256,1024]{1,0:T(8,128)S(1)}, bf16[256,2048]{1,0:T(8,128)(2,1)S(1)}, f32[1,128]{1,0:T(1,128)S(1)}, s32[1,8]{1,0:T(1,128)S(1)}) custom-call(bf16[256,1024]{1,0:T(8,128)(2,1)S(1)} %bitcast.10, bf16[256,1024]{1,0:T(8,128)(2,1)S(1)} %get-tuple-element.37.k_ref, f32[8,256]{1,0:T(8,128)S(1)} %get-tuple-element.38.beta_ref, ...), custom_call_target="tpu_custom_call" | custom-call | flops 2147483648 | bytes 4194304 | tf_op jit(solution)/shard_map/queries/pallas_call | solution.py:395
  20.0 0.0 collective-permute-done.2.refs_1_
  20.0 0.0 collective-permute-done.1.refs_0_
  20.0 0.4 %enter.1 = (f32[512,128]{1,0:T(8,128)S(1)}, f32[512,128]{1,0:T(8,128)S(1)}) custom-call(s32[1]{0:T(128)} %bitcast.core_ref, bf16[1040,128]{1,0:T(8,128)(2,1)S(1)} %get-tuple-element.33.keep_ref, bf16[1040,128]{1,0:T(8,128)(2,1)S(1)} %collective-permute-done.got_ref, bf16[1040,128]{1,0:T(8,128)(2,1)S(1)} %collective-permute-done.1.refs_0_, ...), custom_call_target="tpu_custom_call" | custom-call | flops 33554432 | bytes 4194304 | tf_op jit(solution)/shard_map/enter/pallas_call | solution.py:401
  20.5 0.1 collective-permute-start.3
  20.5 0.7 %rows_own.1 = (bf16[256,1024]{1,0:T(8,128)(2,1)S(1)}, bf16[8,1024]{1,0:T(8,128)(2,1)S(1)}) custom-call(s32[1]{0:T(128)} %bitcast.core_ref, f32[512,128]{1,0:T(8,128)S(1)} %get-tuple-element.56.state_ref, f32[256,1024]{1,0:T(8,128)S(1)} %get-tuple-element.52.local_ref, bf16[256,2048]{1,0:T(8,128)(2,1)S(1)} %get-tuple-element.53.reach_ref, ...), custom_call_target="tpu_custom_call" | custom-call | flops 2147483648 | bytes 4194304 | tf_op jit(solution)/shard_map/rows_own/pallas_call | solution.py:409
  21.2 0.9 %collective-permute-done.3.state_ref = f32[512,128]{1,0:T(8,128)S(1)} collective-permute-done((f32[512,128]{1,0:T(8,128)S(1)}, f32[512,128]{1,0:T(8,128)S(1)}, u32[]{:S(2)}, u32[]{:S(2)}) %collective-permute-start.3) | collective-permute-done | bytes 262176 | tf_op jit(solution)/shard_map/ppermute | solution.py:374
  22.1 0.6 %rows_other.1 = (bf16[256,1024]{1,0:T(8,128)(2,1)S(1)}, bf16[8,1024]{1,0:T(8,128)(2,1)S(1)}) custom-call(s32[1]{0:T(128)} %bitcast.core_ref, f32[512,128]{1,0:T(8,128)S(1)} %collective-permute-done.3.state_ref, f32[256,1024]{1,0:T(8,128)S(1)} %get-tuple-element.52.local_ref, ...), custom_call_target="tpu_custom_call", output_to_operand_aliasing={{0}: (7, {}), {1}: (8, {})} | custom-call | flops 67108864 | bytes 4194304 | tf_op jit(solution)/shard_map/rows_other/pallas_call | solution.py:412
  22.7 1.5 %collective-permute-start.5 = (bf16[256,1024]{1,0:T(8,128)(2,1)S(1)}, bf16[256,1024]{1,0:T(8,128)(2,1)S(1)}, u32[]{:S(2)}, u32[]{:S(2)}) collective-permute-start(bf16[256,1024]{1,0:T(8,128)(2,1)S(1)} %get-tuple-element.61), channel_id=1, source_target_pairs={{0,1},{1,0},{2,3},{3,2},{4,5},{5,4},{6,7},{7,6},{8,9},{9,8},{10,11... | collective-permute-start | bytes 1572872 | tf_op jit(solution)/shard_map/ppermute | solution.py:416
  24.2 0.0 collective-permute-start.4
  24.2 1.2 %collective-permute-done.4.b_ref = bf16[8,1024]{1,0:T(8,128)(2,1)S(1)} collective-permute-done((bf16[8,1024]{1,0:T(8,128)(2,1)S(1)}, bf16[8,1024]{1,0:T(8,128)(2,1)S(1)}, u32[]{:S(2)}, u32[]{:S(2)}) %collective-permute-start.4) | collective-permute-done | bytes 16416 | tf_op jit(solution)/shard_map/ppermute | solution.py:374
  25.4 15.8 %all_to_all.5.parts_ref = bf16[8,8,1024]{2,1,0:T(8,128)(2,1)S(1)} all-to-all(bf16[8,8,1024]{2,1,0:T(8,128)(2,1)S(1)} %sums.1), channel_id=1, replica_groups={{0,4,8,12,16,20,24,28},{2,6,10,14,18,22,26,30},{1,5,9,13,17,21,25,29},{..., dimensions={0} | all-to-all | bytes 262144 | tf_op jit(solution)/shard_map/all_to_all | solution.py:419
  41.2 0.0 collective-permute-done.5.rows_ref
  41.2 0.9 %final.1 = (f32[1,8]{1,0:T(1,128)}, bf16[256,1024]{1,0:T(8,128)(2,1)}) custom-call(bf16[8,8,1024]{2,1,0:T(8,128)(2,1)S(1)} %all_to_all.5.parts_ref, s32[1,8]{1,0:T(1,128)S(1)} %get-tuple-element.60.pos_ref, bf16[256,1024]{1,0:T(8,128)(2,1)S(1)} %collective-permute-done.5.rows_ref), custom_call_target="tpu_custom_call" | custom-call | tf_op jit(solution)/shard_map/final/pallas_call | solution.py:421
  (1 shorter events, 0.0 us)
Async XLA Ops:
  6.4 10.3 %copy-start = (bf16[1,1,256,1024]{3,2,1,0:T(8,128)(2,1)S(1)}, bf16[1,1,256,1024]{3,2,1,0:T(8,128)(2,1)}, u32[]{:S(2)}) copy-start(bf16[1,1,256,1024]{3,2,1,0:T(8,128)(2,1)} %param.9) | copy-start | bytes 1572868
  6.4 1.7 %collective-permute-start = (bf16[1040,128]{1,0:T(8,128)(2,1)S(1)}, bf16[1040,128]{1,0:T(8,128)(2,1)S(1)}, u32[]{:S(2)}, u32[]{:S(2)}) collective-permute-start(bf16[1040,128]{1,0:T(8,128)(2,1)S(1)} %get-tuple-element.34), channel_id=1, source_target_pairs={{0,2},{2,0},{4,6},{6,4},{8,10},{10,8},{12,14},{14,12},{16,18},{18,... | collective-permute-start | bytes 798728 | tf_op jit(solution)/shard_map/ppermute | solution.py:374
  8.3 11.7 %collective-permute-start.1 = (bf16[1040,128]{1,0:T(8,128)(2,1)S(1)}, bf16[1040,128]{1,0:T(8,128)(2,1)S(1)}, u32[]{:S(2)}, u32[]{:S(2)}) collective-permute-start(bf16[1040,128]{1,0:T(8,128)(2,1)S(1)} %get-tuple-element.35), channel_id=1, source_target_pairs={{0,4},{2,6},{4,8},{6,10},{8,12},{10,14},{12,16},{14,18},{16,20},{1... | collective-permute-start | bytes 798728 | tf_op jit(solution)/shard_map/ppermute | solution.py:377
  13.1 6.9 %collective-permute-start.2 = (bf16[528,128]{1,0:T(8,128)(2,1)S(1)}, bf16[528,128]{1,0:T(8,128)(2,1)S(1)}, u32[]{:S(2)}, u32[]{:S(2)}) collective-permute-start(bf16[528,128]{1,0:T(8,128)(2,1)S(1)} %get-tuple-element.36), channel_id=1, source_target_pairs={{0,8},{2,10},{4,12},{6,14},{8,16},{10,18},{12,20},{14,22},{16,24},... | collective-permute-start | bytes 405512 | tf_op jit(solution)/shard_map/ppermute | solution.py:377
  16.6 0.7 %copy-start.1 = (f32[1,128]{1,0:T(1,128)S(1)}, f32[1,128]{1,0:T(1,128)}, u32[]{:S(2)}) copy-start(f32[1,128]{1,0:T(1,128)} %gain_in.1) | copy-start | bytes 1540
  16.6 0.7 %copy-start.2 = (s32[1,1,8]{2,1,0:T(1,128)S(1)}, s32[1,1,8]{2,1,0:T(1,128)}, u32[]{:S(2)}) copy-start(s32[1,1,8]{2,1,0:T(1,128)} %param.14) | copy-start | bytes 100
  20.5 1.6 %collective-permute-start.3 = (f32[512,128]{1,0:T(8,128)S(1)}, f32[512,128]{1,0:T(8,128)S(1)}, u32[]{:S(2)}, u32[]{:S(2)}) collective-permute-start(f32[512,128]{1,0:T(8,128)S(1)} %get-tuple-element.51), channel_id=1, source_target_pairs={{0,2},{2,0},{4,6},{6,4},{8,10},{10,8},{12,14},{14,12},{16,18},{18,... | collective-permute-start | bytes 786440 | tf_op jit(solution)/shard_map/ppermute | solution.py:374
  22.7 18.5 %collective-permute-start.5 = (bf16[256,1024]{1,0:T(8,128)(2,1)S(1)}, bf16[256,1024]{1,0:T(8,128)(2,1)S(1)}, u32[]{:S(2)}, u32[]{:S(2)}) collective-permute-start(bf16[256,1024]{1,0:T(8,128)(2,1)S(1)} %get-tuple-element.61), channel_id=1, source_target_pairs={{0,1},{1,0},{2,3},{3,2},{4,5},{5,4},{6,7},{7,6},{8,9},{9,8},{10,11... | collective-permute-start | bytes 1572872 | tf_op jit(solution)/shard_map/ppermute | solution.py:416
  24.2 1.2 %collective-permute-start.4 = (bf16[8,1024]{1,0:T(8,128)(2,1)S(1)}, bf16[8,1024]{1,0:T(8,128)(2,1)S(1)}, u32[]{:S(2)}, u32[]{:S(2)}) collective-permute-start(bf16[8,1024]{1,0:T(8,128)(2,1)S(1)} %get-tuple-element.59.a_ref), channel_id=1, source_target_pairs={{0,2},{2,0},{4,6},{6,4},{8,10},{10,8},{12,14},{14,12},{16,18},{18,... | collective-permute-start | bytes 49160 | tf_op jit(solution)/shard_map/ppermute | solution.py:374
